TPU v7x, 32 devices: a whole 2x2x4 slice. The times are simulated.
32 devices in a mesh: ctx: 8 (over z, y), head: 4 (over x, core).
Axes of the slice: x: 2, y: 2, z: 4, core: 2. Of those that a mesh axis runs over, the one named last changes fastest.
Arguments:
- norm_out: bfloat16 [1152, 4096], P('ctx'), may hold values from -1.75 to 1.75
- out_grad: bfloat16 [1152, 512], P('ctx', 'head'), may hold values from -6 to 6
- attn_out: bfloat16 [1152, 512], P('ctx', 'head'), may hold values from -12 to 12
- log_norm: float32 [4, 1152], P('head', 'ctx'), may hold values from 5.5 to 7.5
- query_weight: bfloat16 [4096, 512], P(None, 'head'), may hold values from -0.09375 to 0.09375
- key_weight: bfloat16 [4096, 128], P(None, 'head'), may hold values from -0.09375 to 0.09375
- value_weight: bfloat16 [4096, 128], P(None, 'head'), may hold values from -0.09375 to 0.09375
- span_order: int32 [16], replicated, may hold values from 0 to 15, each once
Outputs:
- input_grad: bfloat16 [1152, 4096], P(('ctx', 'head'))
Inputs may be any that keep to these rules, and one draw needn't show every extreme that they name: Shard c holds block span_order[2 c] in its first 72 rows and span_order[2 c + 1] in the rest; each of the 16 blocks once.
All inputs are finite; a program needn't handle non-finite values.
Results may differ from a plain program's by a relative error of at most 0.015.
Values may be sent and summed in bfloat16 or wider, within the bound.
No kernel may reach another device: no remote copies, remote signals or barrier semaphores. Data moves between devices by JAX's collectives and lax.ppermute only.
A program may use at most 64 MiB of HBM per device.

v0:
```python
import functools

import jax
import jax.numpy as jnp
from jax import lax
from jax.experimental import pallas as pl
from jax.experimental.pallas import tpu as pltpu
from jax.sharding import PartitionSpec as P


GROUP = 4
EXTRA = 8
CUTS = 4
GRANT = 16 * 2**20
F32 = jnp.float32
BF16 = jnp.bfloat16


def nn(left, right):
    return jnp.dot(left, right, preferred_element_type=F32)


def nt(left, right):
    return lax.dot_general(left, right, (((1,), (1,)), ((), ())), preferred_element_type=F32)


def tn(left, right):
    return lax.dot_general(left, right, (((0,), (0,)), ((), ())), preferred_element_type=F32)


def three_pieces(row):
    high = row.astype(BF16).astype(F32)
    rest = row - high
    middle = rest.astype(BF16).astype(F32)
    return high, middle, rest - middle


def first_kernel(
    norm_hbm, wq_hbm, kw_hbm, vw_hbm, grad_hbm, attn_hbm, lse_hbm,
    side_ref, norm_ref, wkv_ref, wq_ref, grad_ref, attn_ref, lse_ref, sems,
):
    rows, depth = norm_ref.shape
    width = wq_ref.shape[1]
    quarter = wkv_ref.shape[0] // 2
    cut = depth // CUTS

    def fetch(at, source, target):
        copy = pltpu.make_async_copy(source, target, sems.at[at])
        copy.start()
        return copy

    norms, weights = [], []
    for k in range(CUTS):
        part = slice(k * cut, (k + 1) * cut)
        norms.append(fetch(2 * k, norm_hbm.at[:, part], norm_ref.at[:, part]))
        weights.append(fetch(2 * k + 1, wq_hbm.at[part, :], wq_ref.at[part, :]))
    at = 2 * CUTS
    others = [
        fetch(at, grad_hbm, grad_ref),
        fetch(at + 1, attn_hbm, attn_ref),
        fetch(at + 2, lse_hbm, lse_ref),
        fetch(at + 3, kw_hbm, wkv_ref.at[0:quarter, :]),
        fetch(at + 4, vw_hbm, wkv_ref.at[quarter : 2 * quarter, :]),
    ]
    query = jnp.zeros((rows, width), F32)
    for k in range(CUTS):
        part = slice(k * cut, (k + 1) * cut)
        norms[k].wait()
        weights[k].wait()
        query = query + nn(norm_ref[:, part], wq_ref[part, :])
    for copy in others:
        copy.wait()
    grad = grad_ref[...]
    prod = grad.astype(F32) * attn_ref[...].astype(F32)
    high = prod.astype(BF16)
    low = (prod - high.astype(F32)).astype(BF16)
    ones = jnp.ones((8, width), BF16)
    delta = (nt(ones, high) + nt(ones, low))[0:1, :]
    index = lax.broadcasted_iota(jnp.int32, (EXTRA, rows), 0)
    extra = jnp.zeros((EXTRA, rows), F32)
    for at, piece in enumerate(three_pieces(lse_ref[...]) + three_pieces(delta)):
        extra = jnp.where(index == at, piece, extra)
    side_ref[0:rows, 0:width] = query.astype(BF16)
    side_ref[0:rows, width:] = grad
    side_ref[rows:, :] = jnp.zeros((EXTRA, 2 * width), BF16)
    side_ref[rows:, 0:rows] = extra.astype(BF16)


def second_kernel(norm_ref, wkv_ref, kw2_ref, vw2_ref, side_ref, keyval_ref, far_ref):
    rows, width = keyval_ref.shape
    odd = lax.axis_index("ctx") % 2 == 1
    pair = jnp.concatenate([wkv_ref[...], kw2_ref[...], vw2_ref[...]], axis=0)
    keyval = nt(norm_ref[...], pair).astype(BF16)
    keyval_ref[...] = keyval

    @pl.when(odd)
    def _():
        far_ref[0:rows, 0:width] = keyval
        far_ref[0:rows, width:] = keyval
        far_ref[rows:, :] = jnp.zeros((EXTRA, 2 * width), BF16)

    @pl.when(jnp.logical_not(odd))
    def _():
        far_ref[...] = side_ref[...]


def stack_kernel(*refs):
    out_ref = refs[-1]
    at = 0
    for ref in refs[:-1]:
        out_ref[at : at + ref.shape[0], :] = ref[...]
        at += ref.shape[0]


def third_kernel(own_ref, near_ref, far_ref, out_ref):
    rows, width = own_ref.shape
    odd = lax.axis_index("ctx") % 2 == 1
    out_ref[0:rows, :] = own_ref[...]

    @pl.when(odd)
    def _():
        out_ref[rows:, :] = near_ref[...]

    @pl.when(jnp.logical_not(odd))
    def _():
        out_ref[rows:, :] = far_ref[0:rows, 0:width]


def local(body, outs, args, spaces=None, scratch=()):
    spaces = spaces or [pltpu.VMEM] * len(args)
    vmem = pl.BlockSpec(memory_space=pltpu.VMEM)
    many = isinstance(outs, tuple)
    shapes = tuple(jax.ShapeDtypeStruct(*o) for o in outs) if many else jax.ShapeDtypeStruct(*outs[0])
    args = [
        pltpu.with_memory_space_constraint(a, pltpu.HBM) if space is pltpu.HBM else a
        for a, space in zip(args, spaces)
    ]
    return pl.pallas_call(
        body,
        out_shape=shapes,
        in_specs=[pl.BlockSpec(memory_space=space) for space in spaces],
        out_specs=tuple(vmem for _ in outs) if many else vmem,
        scratch_shapes=list(scratch),
        compiler_params=pltpu.CompilerParams(vmem_limit_bytes=GRANT),
    )(*args)


def attention_kernel(
    span_ref, side_ref, near_ref, far_ref, later_ref, kva1_ref, kvx1_ref, kva2_ref, kvx2_ref, out_ref
):
    padded = side_ref.shape[0]
    rows = padded - EXTRA
    half = rows // 2
    width = kva1_ref.shape[1]
    quarter = width // GROUP
    scale = width ** (-0.5)
    shards = lax.axis_size("ctx")
    here = lax.axis_index("ctx")
    odd = here % 2 == 1
    member = lax.axis_index("head") % GROUP

    source = lax.broadcasted_iota(jnp.int32, (width, 2 * width), 0)
    target = lax.broadcasted_iota(jnp.int32, (width, 2 * width), 1)
    place = ((source // quarter) ^ member) * (2 * quarter) + source % quarter
    put_key = jnp.where(target == place, F32(1.0), F32(0.0)).astype(BF16)
    put_value = jnp.where(target == place + quarter, F32(1.0), F32(0.0)).astype(BF16)

    def positions(shard, axis):
        shape = (rows, 1) if axis == 0 else (1, rows)
        index = lax.broadcasted_iota(jnp.int32, shape, axis)
        first = span_ref[2 * shard]
        second = span_ref[2 * shard + 1]
        return jnp.where(index < half, first * half + index, (second - 1) * half + index)

    def queries(block, shard):
        spread = nn(block[0:rows, 0:width], put_key).astype(BF16)
        grad = nn(block[0:rows, width : 2 * width], put_value).astype(BF16)
        tail = block[rows : rows + 8, :].astype(F32)
        lse = tail[0:1, 0:rows] + tail[1:2, 0:rows] + tail[2:3, 0:rows]
        delta = tail[3:4, 0:rows] + tail[4:5, 0:rows] + tail[5:6, 0:rows]
        return spread, grad, lse, delta, positions(shard, 1)

    def keys(kva_ref, kvx_ref, at, shard):
        part = slice(at * rows, (at + 1) * rows)
        return jnp.concatenate([kva_ref[part, :], kvx_ref[part, :]], axis=1), positions(shard, 0)

    def block(query, key):
        spread, grad, lse, delta, query_pos = query
        keyval, key_pos = key
        scores = nt(keyval, spread) * scale
        prob = jnp.where(key_pos <= query_pos, jnp.exp(scores - lse), F32(0.0))
        dscore = prob * (nt(keyval, grad) - delta)
        return prob.astype(BF16), dscore.astype(BF16)

    def ring(shard):
        return (shard + 2 * shards) % shards

    before = ring(here - 2)
    after = ring(here + 2)
    flip = 1 - 2 * (here % 2)
    own_query = queries(side_ref[...], here)
    own_key = keys(kva1_ref, kvx1_ref, 0, here)

    prob, dscore = block(own_query, own_key)
    dquery = tn(dscore, own_key[0])
    dkey = nn(dscore, own_query[0])
    dvalue = nn(prob, own_query[1])
    for kva_ref, kvx_ref, at, shard in (
        (kva1_ref, kvx1_ref, 1, ring(jnp.where(odd, here - 1, here - 3))),
        (kva2_ref, kvx2_ref, 0, before),
        (kva2_ref, kvx2_ref, 1, ring(before + flip)),
    ):
        key = keys(kva_ref, kvx_ref, at, shard)
        _, dscore = block(own_query, key)
        dquery += tn(dscore, key[0])
    third = jnp.where(odd, far_ref[...], near_ref[...])
    for packed, shard in (
        (later_ref[0:padded, :], after),
        (later_ref[padded:, :], ring(after + flip)),
        (third, ring(jnp.where(odd, here + 3, here + 1))),
    ):
        query = queries(packed, shard)
        prob, dscore = block(query, own_key)
        dkey += nn(dscore, query[0])
        dvalue += nn(prob, query[1])
    dquery_b = (dquery * scale).astype(BF16)
    out_ref[:, 0:width] = nt(dquery_b, put_key).astype(BF16)
    out_ref[:, width:] = (dkey * scale + dvalue).astype(BF16)


def split_kernel(mine, grads_ref, send_ref, keep_ref):
    rows, columns = grads_ref.shape
    width = columns // 3
    padded = send_ref.shape[0] // 2
    member = lax.axis_index("head")
    grads = grads_ref[...]
    slot = lax.broadcasted_iota(jnp.int32, (padded, rows), 0)
    token = lax.broadcasted_iota(jnp.int32, (padded, rows), 1)

    def rows_of(owner):
        chosen = jnp.where((token == owner * mine + slot) & (slot < mine), F32(1.0), F32(0.0))
        return nn(chosen.astype(BF16), grads)

    for at, (other, kept) in enumerate(((3, 2), (1, 0))):
        part = slice(at * padded, (at + 1) * padded)
        keep_ref[part, :] = rows_of(member ^ kept).astype(BF16)
        sent = rows_of(member ^ other)
        send_ref[part, 0:width] = sent[:, 0:width].astype(BF16)
        for step in (1, 2):
            lanes = slice(step * width, (step + 1) * width)
            send_ref[part, lanes] = pltpu.roll(sent[:, lanes], width // 2, 1).astype(BF16)


def term_kernel(at, keep_ref, got_ref, wq_ref, wq2_ref, *refs):
    weights, out_ref = refs[:-1], refs[-1]
    mine, depth = out_ref.shape
    width = wq_ref.shape[1]
    padded = keep_ref.shape[0] // 2
    part = slice(at * padded, (at + 1) * padded)
    keep = keep_ref[part, :]
    got = got_ref[part, :]
    both = (keep[:, width:].astype(F32) + got[:, width:].astype(F32)).astype(BF16)
    cut = depth // CUTS
    for k in range(CUTS):
        cols = slice(k * cut, (k + 1) * cut)
        total = nt(keep[:, 0:width], wq_ref[cols, :]) + nt(got[:, 0:width], wq2_ref[cols, :])
        stacked = jnp.concatenate([w[:, cols] for w in weights], axis=0)
        total = total + nn(both, stacked)
        out_ref[:, cols] = total[0:mine, :].astype(out_ref.dtype)


def per_device(
    norm_out, out_grad, attn_out, log_norm, query_weight, key_weight, value_weight, span_order
):
    shards = lax.axis_size("ctx")
    heads = lax.axis_size("head")
    rows = norm_out.shape[0]
    width = query_weight.shape[1]

    def sent(array, axis, to):
        return lax.ppermute(array, axis, [(i, to(i)) for i in range(lax.axis_size(axis))])

    def flipped(array, axis, bit):
        return sent(array, axis, lambda i: i ^ bit)

    def shifted(array, by):
        return sent(array, "ctx", lambda i: (i + by) % shards)

    kw, vw = key_weight.T, value_weight.T
    quarter, depth = kw.shape
    kw2, vw2 = flipped(kw, "head", 1), flipped(vw, "head", 1)
    wq2 = flipped(query_weight, "head", 1)
    tall = rows + EXTRA
    side, norm, wkv = local(
        first_kernel,
        (((tall, 2 * width), BF16), ((rows, depth), BF16), ((2 * quarter, depth), BF16)),
        (norm_out, query_weight, kw, vw, out_grad, attn_out, log_norm),
        [pltpu.HBM] * 7,
        [
            pltpu.VMEM((depth, width), BF16),
            pltpu.VMEM((rows, width), BF16),
            pltpu.VMEM((rows, width), BF16),
            pltpu.VMEM((1, rows), F32),
            pltpu.SemaphoreType.DMA((2 * CUTS + 5,)),
        ],
    )
    wkv3 = flipped(wkv, "head", 2)
    keyval, far = local(
        second_kernel,
        (((rows, width), BF16), ((tall, 2 * width), BF16)),
        (norm, wkv, kw2, vw2, side),
    )
    near_kv = flipped(keyval, "ctx", 1)
    near = flipped(side, "ctx", 1)
    far = sent(far, "ctx", lambda i: (i + (3 if i % 2 else -3)) % shards)
    pair_kv = local(stack_kernel, [((2 * rows, width), BF16)], (keyval, near_kv))
    kva2 = shifted(pair_kv, 2)
    pair_side = local(stack_kernel, [((2 * tall, 2 * width), BF16)], (side, near))
    later = shifted(pair_side, -2)
    kva1 = local(third_kernel, [((2 * rows, width), BF16)], (keyval, near_kv, far))
    kvx1 = flipped(kva1, "head", 2)
    kvx2 = flipped(kva2, "head", 2)
    wkv4 = flipped(wkv3, "head", 1)
    weights = (wkv, kw2, vw2, wkv3, wkv4)
    grads = local(
        attention_kernel,
        [((rows, 3 * width), BF16)],
        (span_order, side, near, far, later, kva1, kvx1, kva2, kvx2),
        [pltpu.SMEM] + [pltpu.VMEM] * 8,
    )
    if heads != GROUP:
        full = nt(grads[:, :width], query_weight)
        full = full + nn(grads[:, width:], jnp.concatenate(weights, axis=0))
        return lax.psum_scatter(full.astype(BF16), "head", scatter_dimension=0, tiled=True)
    mine = rows // heads
    padded = -(-mine // 8) * 8
    block = ((2 * padded, 3 * width), BF16)
    send, keep = local(functools.partial(split_kernel, mine), (block, block), (grads,))
    got = flipped(send, "head", 1)
    operands = (keep, got, query_weight, wq2) + weights
    away = local(functools.partial(term_kernel, 0), [((mine, depth), BF16)], operands)
    arrived = flipped(away, "head", 2)
    stay = local(functools.partial(term_kernel, 1), [((mine, depth), F32)], operands)
    return (stay + arrived.astype(F32)).astype(BF16)


def solution(mesh):
    in_specs = (
        P("ctx", None),
        P("ctx", "head"),
        P("ctx", "head"),
        P("head", "ctx"),
        P(None, "head"),
        P(None, "head"),
        P(None, "head"),
        P(),
    )
    out_specs = P(("ctx", "head"), None)

    return jax.shard_map(
        per_device, mesh=mesh, in_specs=in_specs, out_specs=out_specs, check_vma=False
    )
```

profile of v0, /device:TPU:0, one launch (start us, length us, event | category | flops | bytes accessed | tf_op | source)
XLA Modules:
  0.0 57.8 jit_solution(2310985549620600905)
XLA Ops:
  0.0 0.5 collective-permute-start.10
  0.5 0.0 copy-start.2
  0.5 0.0 copy-start.3
  0.5 2.3 %shard_map.82 = (bf16[152,256]{1,0:T(8,128)(2,1)S(1)}, bf16[144,4096]{1,0:T(8,128)(2,1)S(1)}, bf16[64,4096]{1,0:T(8,128)(2,1)S(1)}) custom-call(bf16[144,4096]{1,0:T(8,128)(2,1)} %norm_hbm.1, bf16[4096,128]{1,0:T(8,128)(2,1)} %wq_ref.3, bf16[32,4096]{1,0:T(8,128)(2,1)} %bitcast.2, bf16[32,4096]{1,0:T(8,128)(2,1)} %bitcast.4, bf16[144,128]{1,0:T(8,128)(2,1)} %grad_hbm.1, ...), custom_call_target="tpu_custom_call" | custom-call | tf_op jit(solution)/shard_map/pallas_call | solution.py:138
  2.8 2.5 %collective-permute-start.11 = (bf16[64,4096]{1,0:T(8,128)(2,1)S(1)}, bf16[64,4096]{1,0:T(8,128)(2,1)S(1)}, u32[]{:S(2)}, u32[]{:S(2)}) collective-permute-start(bf16[64,4096]{1,0:T(8,128)(2,1)S(1)} %get-tuple-element.14.wkv_ref.refs_0_), channel_id=1, source_target_pairs={{0,2},{1,3},{2,0},{3,1},{4,6},{5,7},{6,4},{7,5},{8,10},{9,11},{10,... | collective-permute-start | bytes 1572872 | tf_op jit(solution)/shard_map/ppermute | solution.py:281
  5.4 12.6 %collective-permute-done.11.refs_3_ = bf16[64,4096]{1,0:T(8,128)(2,1)S(1)} collective-permute-done((bf16[64,4096]{1,0:T(8,128)(2,1)S(1)}, bf16[64,4096]{1,0:T(8,128)(2,1)S(1)}, u32[]{:S(2)}, u32[]{:S(2)}) %collective-permute-start.11) | collective-permute-done | bytes 524320 | tf_op jit(solution)/shard_map/ppermute | solution.py:281
  18.0 0.0 collective-permute-start.12
  18.0 0.0 copy-done.2
  18.0 0.5 collective-permute-start.1
  18.5 0.0 copy-done.3
  18.5 0.1 collective-permute-start.2
  18.6 1.8 %collective-permute-start = (bf16[152,256]{1,0:T(8,128)(2,1)S(1)}, bf16[152,256]{1,0:T(8,128)(2,1)S(1)}, u32[]{:S(2)}, u32[]{:S(2)}) collective-permute-start(bf16[152,256]{1,0:T(8,128)(2,1)S(1)} %get-tuple-element.12.side_ref.refs_0_), channel_id=1, source_target_pairs={{0,4},{4,0},{8,12},{12,8},{16,20},{20,16},{24,28},{28,24},{1,5},{5... | collective-permute-start | bytes 233480 | tf_op jit(solution)/shard_map/ppermute | solution.py:281
  20.3 0.0 collective-permute-done.1.kw2_ref.refs_1_
  20.3 0.3 collective-permute-done.2.vw2_ref.refs_2_
  20.6 0.0 copy-start.1
  20.6 0.5 shard_map.83
  21.1 0.0 copy-start
  21.2 1.8 %collective-permute-start.5 = (bf16[144,128]{1,0:T(8,128)(2,1)S(1)}, bf16[144,128]{1,0:T(8,128)(2,1)S(1)}, u32[]{:S(2)}, u32[]{:S(2)}) collective-permute-start(bf16[144,128]{1,0:T(8,128)(2,1)S(1)} %get-tuple-element.16.own_ref.refs_0_), channel_id=1, source_target_pairs={{0,4},{4,0},{8,12},{12,8},{16,20},{20,16},{24,28},{28,24},{1,5},{5... | collective-permute-start | bytes 110600 | tf_op jit(solution)/shard_map/ppermute | solution.py:281
  23.0 0.3 collective-permute-done.refs_1_.near_ref
  23.3 3.9 %collective-permute-start.4 = (bf16[304,256]{1,0:T(8,128)(2,1)S(1)}, bf16[304,256]{1,0:T(8,128)(2,1)S(1)}, u32[]{:S(2)}, u32[]{:S(2)}) collective-permute-start(bf16[304,256]{1,0:T(8,128)(2,1)S(1)} %shard_map.84), channel_id=1, source_target_pairs={{0,24},{4,28},{8,0},{12,4},{16,8},{20,12},{24,16},{28,20},{1,25},{... | collective-permute-start | bytes 466952 | tf_op jit(solution)/shard_map/ppermute | solution.py:281
  27.2 0.4 collective-permute-start.3
  27.6 0.0 collective-permute-done.5.near_ref.refs_1_
  27.6 1.6 %collective-permute-start.7 = (bf16[288,128]{1,0:T(8,128)(2,1)S(1)}, bf16[288,128]{1,0:T(8,128)(2,1)S(1)}, u32[]{:S(2)}, u32[]{:S(2)}) collective-permute-start(bf16[288,128]{1,0:T(8,128)(2,1)S(1)} %shard_map.86), channel_id=1, source_target_pairs={{0,8},{4,12},{8,16},{12,20},{16,24},{20,28},{24,0},{28,4},{1,9},{5... | collective-permute-start | bytes 221192 | tf_op jit(solution)/shard_map/ppermute | solution.py:281
  29.2 6.8 %collective-permute-done.3.far_ref = bf16[152,256]{1,0:T(8,128)(2,1)S(1)} collective-permute-done((bf16[152,256]{1,0:T(8,128)(2,1)S(1)}, bf16[152,256]{1,0:T(8,128)(2,1)S(1)}, u32[]{:S(2)}, u32[]{:S(2)}) %collective-permute-start.3) | collective-permute-done | bytes 77856 | tf_op jit(solution)/shard_map/ppermute | solution.py:281
  36.0 1.6 %collective-permute-start.6 = (bf16[288,128]{1,0:T(8,128)(2,1)S(1)}, bf16[288,128]{1,0:T(8,128)(2,1)S(1)}, u32[]{:S(2)}, u32[]{:S(2)}) collective-permute-start(bf16[288,128]{1,0:T(8,128)(2,1)S(1)} %shard_map.85.kva1_ref), channel_id=1, source_target_pairs={{0,2},{1,3},{2,0},{3,1},{4,6},{5,7},{6,4},{7,5},{8,10},{9,11},{10,... | collective-permute-start | bytes 221192 | tf_op jit(solution)/shard_map/ppermute | solution.py:281
  37.6 0.0 collective-permute-done.7.kva2_ref
  37.6 0.5 collective-permute-start.8
  38.1 0.0 collective-permute-done.4.later_ref
  38.1 2.3 %collective-permute-done.6.kvx1_ref = bf16[288,128]{1,0:T(8,128)(2,1)S(1)} collective-permute-done((bf16[288,128]{1,0:T(8,128)(2,1)S(1)}, bf16[288,128]{1,0:T(8,128)(2,1)S(1)}, u32[]{:S(2)}, u32[]{:S(2)}) %collective-permute-start.6) | collective-permute-done | bytes 73760 | tf_op jit(solution)/shard_map/ppermute | solution.py:281
  40.4 1.5 %collective-permute-done.8.kvx2_ref = bf16[288,128]{1,0:T(8,128)(2,1)S(1)} collective-permute-done((bf16[288,128]{1,0:T(8,128)(2,1)S(1)}, bf16[288,128]{1,0:T(8,128)(2,1)S(1)}, u32[]{:S(2)}, u32[]{:S(2)}) %collective-permute-start.8) | collective-permute-done | bytes 73760 | tf_op jit(solution)/shard_map/ppermute | solution.py:281
  41.9 0.0 copy-done.1
  41.9 2.5 %shard_map.87.grads_ref = bf16[144,384]{1,0:T(8,128)(2,1)S(1)} custom-call(s32[16]{0:T(128)S(1)} %copy-done.1, bf16[152,256]{1,0:T(8,128)(2,1)S(1)} %get-tuple-element.12.side_ref.refs_0_, bf16[152,256]{1,0:T(8,128)(2,1)S(1)} %collective-permute-done.refs_1_.near_ref, bf16[152,256]{1,0:T(8,128)(2,1)S(1)} %collective-permute-done.3.far_ref, ...), custom_call_target="tpu_custom_call" | custom-call | tf_op jit(solution)/shard_map/pallas_call | solution.py:138
  44.4 0.3 shard_map.88
  44.7 0.1 collective-permute-start.9
  44.7 1.2 %collective-permute-done.9.got_ref = bf16[80,384]{1,0:T(8,128)(2,1)S(1)} collective-permute-done((bf16[80,384]{1,0:T(8,128)(2,1)S(1)}, bf16[80,384]{1,0:T(8,128)(2,1)S(1)}, u32[]{:S(2)}, u32[]{:S(2)}) %collective-permute-start.9) | collective-permute-done | bytes 61472 | tf_op jit(solution)/shard_map/ppermute | solution.py:281
  46.0 0.0 collective-permute-done.10.wq2_ref
  46.0 0.0 collective-permute-done.12.refs_4_
  46.0 0.0 copy-done
  46.0 1.2 %shard_map.90 = bf16[36,4096]{1,0:T(8,128)(2,1)S(1)} custom-call(bf16[80,384]{1,0:T(8,128)(2,1)S(1)} %get-tuple-element.17.keep_ref, bf16[80,384]{1,0:T(8,128)(2,1)S(1)} %collective-permute-done.9.got_ref, bf16[4096,128]{1,0:T(8,128)(2,1)S(1)} %copy-done, bf16[4096,128]{1,0:T(8,128)(2,1)S(1)} %collective-permute-done.10.wq2_ref, ...), custom_call_target="tpu_custom_call" | custom-call | tf_op jit(solution)/shard_map/pallas_call | solution.py:138
  47.2 0.9 %collective-permute-start.13 = (bf16[36,4096]{1,0:T(8,128)(2,1)S(1)}, bf16[36,4096]{1,0:T(8,128)(2,1)S(1)}, u32[]{:S(2)}, u32[]{:S(2)}) collective-permute-start(bf16[36,4096]{1,0:T(8,128)(2,1)S(1)} %shard_map.90), channel_id=1, source_target_pairs={{0,2},{1,3},{2,0},{3,1},{4,6},{5,7},{6,4},{7,5},{8,10},{9,11},{10,... | collective-permute-start | bytes 884744 | tf_op jit(solution)/shard_map/ppermute | solution.py:281
  48.1 1.2 %shard_map.89 = f32[36,4096]{1,0:T(8,128)S(1)} custom-call(bf16[80,384]{1,0:T(8,128)(2,1)S(1)} %get-tuple-element.17.keep_ref, bf16[80,384]{1,0:T(8,128)(2,1)S(1)} %collective-permute-done.9.got_ref, bf16[4096,128]{1,0:T(8,128)(2,1)S(1)} %copy-done, bf16[4096,128]{1,0:T(8,128)(2,1)S(1)} %collective-permute-done.10.wq2_ref, ...), custom_call_target="tpu_custom_call" | custom-call | tf_op jit(solution)/shard_map/pallas_call | solution.py:138
  49.2 7.8 %collective-permute-done.13 = bf16[36,4096]{1,0:T(8,128)(2,1)S(1)} collective-permute-done((bf16[36,4096]{1,0:T(8,128)(2,1)S(1)}, bf16[36,4096]{1,0:T(8,128)(2,1)S(1)}, u32[]{:S(2)}, u32[]{:S(2)}) %collective-permute-start.13) | collective-permute-done | bytes 294944 | tf_op jit(solution)/shard_map/ppermute | solution.py:281
  57.0 0.8 %add_convert_fusion = bf16[36,4096]{1,0:T(8,128)(2,1)} fusion(f32[36,4096]{1,0:T(8,128)S(1)} %shard_map.89, bf16[36,4096]{1,0:T(8,128)(2,1)S(1)} %collective-permute-done.13), kind=kLoop, calls=%fused_computation | loop fusion | flops 442368 | bytes 1179648 | tf_op jit(solution)/shard_map/convert_element_type | solution.py:344
  (3 shorter events, 0.0 us)
Async XLA Ops:
  0.0 46.0 %collective-permute-start.10 = (bf16[4096,128]{1,0:T(8,128)(2,1)}, bf16[4096,128]{1,0:T(8,128)(2,1)S(1)}, u32[]{:S(2)}, u32[]{:S(2)}) collective-permute-start(bf16[4096,128]{1,0:T(8,128)(2,1)} %wq_ref.3), channel_id=1, source_target_pairs={{0,1},{1,0},{2,3},{3,2},{4,5},{5,4},{6,7},{7,6},{8,9},{9,8},{10,11... | collective-permute-start | bytes 3145736 | tf_op jit(solution)/shard_map/ppermute | solution.py:281
  0.5 17.5 %copy-start.2 = (bf16[4096,32]{0,1:T(8,128)(2,1)S(1)}, bf16[4096,32]{0,1:T(8,128)(2,1)}, u32[]{:S(2)}) copy-start(bf16[4096,32]{0,1:T(8,128)(2,1)} %param.13) | copy-start | bytes 786436
  0.5 18.0 %copy-start.3 = (bf16[4096,32]{0,1:T(8,128)(2,1)S(1)}, bf16[4096,32]{0,1:T(8,128)(2,1)}, u32[]{:S(2)}) copy-start(bf16[4096,32]{0,1:T(8,128)(2,1)} %param.14) | copy-start | bytes 786436
  2.8 15.1 %collective-permute-start.11 = (bf16[64,4096]{1,0:T(8,128)(2,1)S(1)}, bf16[64,4096]{1,0:T(8,128)(2,1)S(1)}, u32[]{:S(2)}, u32[]{:S(2)}) collective-permute-start(bf16[64,4096]{1,0:T(8,128)(2,1)S(1)} %get-tuple-element.14.wkv_ref.refs_0_), channel_id=1, source_target_pairs={{0,2},{1,3},{2,0},{3,1},{4,6},{5,7},{6,4},{7,5},{8,10},{9,11},{10,... | collective-permute-start | bytes 1572872 | tf_op jit(solution)/shard_map/ppermute | solution.py:281
  18.0 28.0 %collective-permute-start.12 = (bf16[64,4096]{1,0:T(8,128)(2,1)S(1)}, bf16[64,4096]{1,0:T(8,128)(2,1)S(1)}, u32[]{:S(2)}, u32[]{:S(2)}) collective-permute-start(bf16[64,4096]{1,0:T(8,128)(2,1)S(1)} %collective-permute-done.11.refs_3_), channel_id=1, source_target_pairs={{0,1},{1,0},{2,3},{3,2},{4,5},{5,4},{6,7},{7,6},{8,9},{9,8},{10,11... | collective-permute-start | bytes 1572872 | tf_op jit(solution)/shard_map/ppermute | solution.py:281
  18.0 2.4 %collective-permute-start.1 = (bf16[32,4096]{1,0:T(8,128)(2,1)S(1)}, bf16[32,4096]{1,0:T(8,128)(2,1)S(1)}, u32[]{:S(2)}, u32[]{:S(2)}) collective-permute-start(bf16[32,4096]{1,0:T(8,128)(2,1)S(1)} %bitcast.3), channel_id=1, source_target_pairs={{0,1},{1,0},{2,3},{3,2},{4,5},{5,4},{6,7},{7,6},{8,9},{9,8},{10,11... | collective-permute-start | bytes 786440 | tf_op jit(solution)/shard_map/ppermute | solution.py:281
  18.5 2.1 %collective-permute-start.2 = (bf16[32,4096]{1,0:T(8,128)(2,1)S(1)}, bf16[32,4096]{1,0:T(8,128)(2,1)S(1)}, u32[]{:S(2)}, u32[]{:S(2)}) collective-permute-start(bf16[32,4096]{1,0:T(8,128)(2,1)S(1)} %bitcast.5), channel_id=1, source_target_pairs={{0,1},{1,0},{2,3},{3,2},{4,5},{5,4},{6,7},{7,6},{8,9},{9,8},{10,11... | collective-permute-start | bytes 786440 | tf_op jit(solution)/shard_map/ppermute | solution.py:281
  18.6 4.7 %collective-permute-start = (bf16[152,256]{1,0:T(8,128)(2,1)S(1)}, bf16[152,256]{1,0:T(8,128)(2,1)S(1)}, u32[]{:S(2)}, u32[]{:S(2)}) collective-permute-start(bf16[152,256]{1,0:T(8,128)(2,1)S(1)} %get-tuple-element.12.side_ref.refs_0_), channel_id=1, source_target_pairs={{0,4},{4,0},{8,12},{12,8},{16,20},{20,16},{24,28},{28,24},{1,5},{5... | collective-permute-start | bytes 233480 | tf_op jit(solution)/shard_map/ppermute | solution.py:281
  20.6 21.3 %copy-start.1 = (s32[16]{0:T(128)S(1)}, s32[16]{0:T(128)}, u32[]{:S(2)}) copy-start(s32[16]{0:T(128)} %span_ref.1) | copy-start | bytes 196
  21.1 24.8 %copy-start = (bf16[4096,128]{1,0:T(8,128)(2,1)S(1)}, bf16[4096,128]{1,0:T(8,128)(2,1)}, u32[]{:S(2)}) copy-start(bf16[4096,128]{1,0:T(8,128)(2,1)} %wq_ref.3) | copy-start | bytes 3145732
  21.2 6.4 %collective-permute-start.5 = (bf16[144,128]{1,0:T(8,128)(2,1)S(1)}, bf16[144,128]{1,0:T(8,128)(2,1)S(1)}, u32[]{:S(2)}, u32[]{:S(2)}) collective-permute-start(bf16[144,128]{1,0:T(8,128)(2,1)S(1)} %get-tuple-element.16.own_ref.refs_0_), channel_id=1, source_target_pairs={{0,4},{4,0},{8,12},{12,8},{16,20},{20,16},{24,28},{28,24},{1,5},{5... | collective-permute-start | bytes 110600 | tf_op jit(solution)/shard_map/ppermute | solution.py:281
  23.3 14.8 %collective-permute-start.4 = (bf16[304,256]{1,0:T(8,128)(2,1)S(1)}, bf16[304,256]{1,0:T(8,128)(2,1)S(1)}, u32[]{:S(2)}, u32[]{:S(2)}) collective-permute-start(bf16[304,256]{1,0:T(8,128)(2,1)S(1)} %shard_map.84), channel_id=1, source_target_pairs={{0,24},{4,28},{8,0},{12,4},{16,8},{20,12},{24,16},{28,20},{1,25},{... | collective-permute-start | bytes 466952 | tf_op jit(solution)/shard_map/ppermute | solution.py:281
  27.2 8.8 %collective-permute-start.3 = (bf16[152,256]{1,0:T(8,128)(2,1)S(1)}, bf16[152,256]{1,0:T(8,128)(2,1)S(1)}, u32[]{:S(2)}, u32[]{:S(2)}) collective-permute-start(bf16[152,256]{1,0:T(8,128)(2,1)S(1)} %get-tuple-element.15), channel_id=1, source_target_pairs={{0,20},{4,16},{8,28},{12,24},{16,4},{20,0},{24,12},{28,8},{1,21},{... | collective-permute-start | bytes 233480 | tf_op jit(solution)/shard_map/ppermute | solution.py:281
  27.6 10.0 %collective-permute-start.7 = (bf16[288,128]{1,0:T(8,128)(2,1)S(1)}, bf16[288,128]{1,0:T(8,128)(2,1)S(1)}, u32[]{:S(2)}, u32[]{:S(2)}) collective-permute-start(bf16[288,128]{1,0:T(8,128)(2,1)S(1)} %shard_map.86), channel_id=1, source_target_pairs={{0,8},{4,12},{8,16},{12,20},{16,24},{20,28},{24,0},{28,4},{1,9},{5... | collective-permute-start | bytes 221192 | tf_op jit(solution)/shard_map/ppermute | solution.py:281
  36.0 4.4 %collective-permute-start.6 = (bf16[288,128]{1,0:T(8,128)(2,1)S(1)}, bf16[288,128]{1,0:T(8,128)(2,1)S(1)}, u32[]{:S(2)}, u32[]{:S(2)}) collective-permute-start(bf16[288,128]{1,0:T(8,128)(2,1)S(1)} %shard_map.85.kva1_ref), channel_id=1, source_target_pairs={{0,2},{1,3},{2,0},{3,1},{4,6},{5,7},{6,4},{7,5},{8,10},{9,11},{10,... | collective-permute-start | bytes 221192 | tf_op jit(solution)/shard_map/ppermute | solution.py:281
  37.6 4.4 %collective-permute-start.8 = (bf16[288,128]{1,0:T(8,128)(2,1)S(1)}, bf16[288,128]{1,0:T(8,128)(2,1)S(1)}, u32[]{:S(2)}, u32[]{:S(2)}) collective-permute-start(bf16[288,128]{1,0:T(8,128)(2,1)S(1)} %collective-permute-done.7.kva2_ref), channel_id=1, source_target_pairs={{0,2},{1,3},{2,0},{3,1},{4,6},{5,7},{6,4},{7,5},{8,10},{9,11},{10,... | collective-permute-start | bytes 221192 | tf_op jit(solution)/shard_map/ppermute | solution.py:281
  44.7 1.3 %collective-permute-start.9 = (bf16[80,384]{1,0:T(8,128)(2,1)S(1)}, bf16[80,384]{1,0:T(8,128)(2,1)S(1)}, u32[]{:S(2)}, u32[]{:S(2)}) collective-permute-start(bf16[80,384]{1,0:T(8,128)(2,1)S(1)} %get-tuple-element.18), channel_id=1, source_target_pairs={{0,1},{1,0},{2,3},{3,2},{4,5},{5,4},{6,7},{7,6},{8,9},{9,8},{10,11... | collective-permute-start | bytes 184328 | tf_op jit(solution)/shard_map/ppermute | solution.py:281
  47.2 9.8 %collective-permute-start.13 = (bf16[36,4096]{1,0:T(8,128)(2,1)S(1)}, bf16[36,4096]{1,0:T(8,128)(2,1)S(1)}, u32[]{:S(2)}, u32[]{:S(2)}) collective-permute-start(bf16[36,4096]{1,0:T(8,128)(2,1)S(1)} %shard_map.90), channel_id=1, source_target_pairs={{0,2},{1,3},{2,0},{3,1},{4,6},{5,7},{6,4},{7,5},{8,10},{9,11},{10,... | collective-permute-start | bytes 884744 | tf_op jit(solution)/shard_map/ppermute | solution.py:281
where the time goes:
time: 58 us; the launch traced here: 57.8 us
  waiting for transfers between devices  32.8 us (57%)
  starting transfers between devices  16.1 us (28%)
  Pallas kernels  8.01 us (14%)
  other arithmetic  0.78 us (1%)
    ppermute x14, waiting for transfers between devices, sent(): lax.ppermute(array, axis, [(i, to(i)) for i in range(lax.axis_size(axis))])  32.8 us
    ppermute x14, starting transfers between devices, sent(): lax.ppermute(array, axis, [(i, to(i)) for i in range(lax.axis_size(axis))])  16.1 us
    pallas_call x9, Pallas kernels, local(): pl.pallas_call(body, out_shape=shapes, in_specs=[pl.BlockSpec(memory_spac...  8.01 us
  transfers between devices with their start and end apart: 14, of which 8 were waited for; matrix products, arithmetic and copies ran while one was open for 0% of the time, Pallas kernels for 12%

commit v1 on v0

--- a/solution.py
+++ b/solution.py
@@ -145,128 +145,149 @@
     )(*args)
 
 
-def attention_kernel(
-    span_ref, side_ref, near_ref, far_ref, later_ref, kva1_ref, kvx1_ref, kva2_ref, kvx2_ref, out_ref
-):
-    padded = side_ref.shape[0]
-    rows = padded - EXTRA
-    half = rows // 2
-    width = kva1_ref.shape[1]
+def ring(shard):
+    shards = lax.axis_size("ctx")
+    return (shard + 2 * shards) % shards
+
+
+def placing(width):
     quarter = width // GROUP
-    scale = width ** (-0.5)
-    shards = lax.axis_size("ctx")
-    here = lax.axis_index("ctx")
-    odd = here % 2 == 1
     member = lax.axis_index("head") % GROUP
-
     source = lax.broadcasted_iota(jnp.int32, (width, 2 * width), 0)
     target = lax.broadcasted_iota(jnp.int32, (width, 2 * width), 1)
     place = ((source // quarter) ^ member) * (2 * quarter) + source % quarter
     put_key = jnp.where(target == place, F32(1.0), F32(0.0)).astype(BF16)
     put_value = jnp.where(target == place + quarter, F32(1.0), F32(0.0)).astype(BF16)
-
-    def positions(shard, axis):
-        shape = (rows, 1) if axis == 0 else (1, rows)
-        index = lax.broadcasted_iota(jnp.int32, shape, axis)
-        first = span_ref[2 * shard]
-        second = span_ref[2 * shard + 1]
-        return jnp.where(index < half, first * half + index, (second - 1) * half + index)
-
-    def queries(block, shard):
-        spread = nn(block[0:rows, 0:width], put_key).astype(BF16)
-        grad = nn(block[0:rows, width : 2 * width], put_value).astype(BF16)
-        tail = block[rows : rows + 8, :].astype(F32)
-        lse = tail[0:1, 0:rows] + tail[1:2, 0:rows] + tail[2:3, 0:rows]
-        delta = tail[3:4, 0:rows] + tail[4:5, 0:rows] + tail[5:6, 0:rows]
-        return spread, grad, lse, delta, positions(shard, 1)
-
-    def keys(kva_ref, kvx_ref, at, shard):
-        part = slice(at * rows, (at + 1) * rows)
-        return jnp.concatenate([kva_ref[part, :], kvx_ref[part, :]], axis=1), positions(shard, 0)
-
-    def block(query, key):
-        spread, grad, lse, delta, query_pos = query
-        keyval, key_pos = key
-        scores = nt(keyval, spread) * scale
-        prob = jnp.where(key_pos <= query_pos, jnp.exp(scores - lse), F32(0.0))
-        dscore = prob * (nt(keyval, grad) - delta)
-        return prob.astype(BF16), dscore.astype(BF16)
-
-    def ring(shard):
-        return (shard + 2 * shards) % shards
-
-    before = ring(here - 2)
-    after = ring(here + 2)
+    return put_key, put_value
+
+
+def positions(span_ref, shard, rows, axis):
+    half = rows // 2
+    shape = (rows, 1) if axis == 0 else (1, rows)
+    index = lax.broadcasted_iota(jnp.int32, shape, axis)
+    first = span_ref[2 * shard]
+    second = span_ref[2 * shard + 1]
+    return jnp.where(index < half, first * half + index, (second - 1) * half + index)
+
+
+def pieces_sum(tail, at, rows):
+    row = tail[at : at + 1, :] + tail[at + 1 : at + 2, :] + tail[at + 2 : at + 3, :]
+    return row[:, 0:rows]
+
+
+def chosen_rows(mine, rows, padded):
+    member = lax.axis_index("head")
+    slot = lax.broadcasted_iota(jnp.int32, (4 * padded, rows), 0)
+    token = lax.broadcasted_iota(jnp.int32, (4 * padded, rows), 1)
+    inside = slot % padded
+    owner = jnp.where(slot < padded, member ^ 3, member ^ 1)
+    owner = jnp.where(slot >= 2 * padded, member ^ 2, owner)
+    owner = jnp.where(slot >= 3 * padded, member, owner)
+    chosen = jnp.where((token == owner * mine + inside) & (inside < mine), F32(1.0), F32(0.0))
+    return chosen.astype(BF16)
+
+
+def attention_kernel(
+    mine, span_ref, side_ref, near_ref, far_ref, later_ref, kva1_ref, kvx1_ref, kva2_ref, kvx2_ref,
+    *outs,
+):
+    padded = side_ref.shape[0]
+    rows = padded - EXTRA
+    width = kva1_ref.shape[1]
+    scale = width ** (-0.5)
+    log2e = 1.4426950408889634
+    here = lax.axis_index("ctx")
+    odd = here % 2 == 1
     flip = 1 - 2 * (here % 2)
-    own_query = queries(side_ref[...], here)
-    own_key = keys(kva1_ref, kvx1_ref, 0, here)
-
-    prob, dscore = block(own_query, own_key)
-    dquery = tn(dscore, own_key[0])
-    dkey = nn(dscore, own_query[0])
-    dvalue = nn(prob, own_query[1])
-    for kva_ref, kvx_ref, at, shard in (
-        (kva1_ref, kvx1_ref, 1, ring(jnp.where(odd, here - 1, here - 3))),
-        (kva2_ref, kvx2_ref, 0, before),
-        (kva2_ref, kvx2_ref, 1, ring(before + flip)),
-    ):
-        key = keys(kva_ref, kvx_ref, at, shard)
-        _, dscore = block(own_query, key)
-        dquery += tn(dscore, key[0])
+    put_key, put_value = placing(width)
+    before, after = ring(here - 2), ring(here + 2)
+    key_shards = (here, ring(jnp.where(odd, here - 1, here - 3)), before, ring(before + flip))
+    query_shards = (here, ring(jnp.where(odd, here + 3, here + 1)), after, ring(after + flip))
+
+    keyval = jnp.concatenate(
+        [
+            jnp.concatenate([kva1_ref[...], kvx1_ref[...]], axis=1),
+            jnp.concatenate([kva2_ref[...], kvx2_ref[...]], axis=1),
+        ],
+        axis=0,
+    )
     third = jnp.where(odd, far_ref[...], near_ref[...])
-    for packed, shard in (
-        (later_ref[0:padded, :], after),
-        (later_ref[padded:, :], ring(after + flip)),
-        (third, ring(jnp.where(odd, here + 3, here + 1))),
-    ):
-        query = queries(packed, shard)
-        prob, dscore = block(query, own_key)
-        dkey += nn(dscore, query[0])
-        dvalue += nn(prob, query[1])
-    dquery_b = (dquery * scale).astype(BF16)
-    out_ref[:, 0:width] = nt(dquery_b, put_key).astype(BF16)
-    out_ref[:, width:] = (dkey * scale + dvalue).astype(BF16)
-
-
-def split_kernel(mine, grads_ref, send_ref, keep_ref):
-    rows, columns = grads_ref.shape
-    width = columns // 3
-    padded = send_ref.shape[0] // 2
-    member = lax.axis_index("head")
-    grads = grads_ref[...]
-    slot = lax.broadcasted_iota(jnp.int32, (padded, rows), 0)
-    token = lax.broadcasted_iota(jnp.int32, (padded, rows), 1)
-
-    def rows_of(owner):
-        chosen = jnp.where((token == owner * mine + slot) & (slot < mine), F32(1.0), F32(0.0))
-        return nn(chosen.astype(BF16), grads)
-
-    for at, (other, kept) in enumerate(((3, 2), (1, 0))):
-        part = slice(at * padded, (at + 1) * padded)
-        keep_ref[part, :] = rows_of(member ^ kept).astype(BF16)
-        sent = rows_of(member ^ other)
-        send_ref[part, 0:width] = sent[:, 0:width].astype(BF16)
-        for step in (1, 2):
-            lanes = slice(step * width, (step + 1) * width)
-            send_ref[part, lanes] = pltpu.roll(sent[:, lanes], width // 2, 1).astype(BF16)
-
-
-def term_kernel(at, keep_ref, got_ref, wq_ref, wq2_ref, *refs):
-    weights, out_ref = refs[:-1], refs[-1]
-    mine, depth = out_ref.shape
+    blocks = (side_ref[...], third, later_ref[0:padded, :], later_ref[padded:, :])
+    spread = nn(jnp.concatenate([b[0:rows, 0:width] for b in blocks], axis=0), put_key)
+    grad = nn(jnp.concatenate([b[0:rows, width:] for b in blocks], axis=0), put_value)
+    spread, grad = spread.astype(BF16), grad.astype(BF16)
+    tails = [b[rows:, :].astype(F32) for b in blocks]
+    lse_row = jnp.concatenate([pieces_sum(t, 0, rows) for t in tails], axis=1)
+    delta_row = jnp.concatenate([pieces_sum(t, 3, rows) for t in tails], axis=1)
+
+    own_tail = blocks[0][rows:, 0:rows]
+    index = lax.broadcasted_iota(jnp.int32, (EXTRA, 128), 0)
+    first_three = jnp.where(index < 3, F32(1.0), F32(0.0)).astype(BF16)
+    next_three = jnp.where((index >= 3) & (index < 6), F32(1.0), F32(0.0)).astype(BF16)
+    lse_col = tn(own_tail, first_three)[:, 0:1]
+    delta_col = tn(own_tail, next_three)[:, 0:1]
+
+    query_pos = positions(span_ref, here, rows, 0)
+    key_pos = jnp.concatenate([positions(span_ref, s, rows, 1) for s in key_shards], axis=1)
+    scores = nt(spread[0:rows], keyval) * (scale * log2e)
+    prob = jnp.where(key_pos <= query_pos, jnp.exp2(scores - lse_col * log2e), F32(0.0))
+    dscore = prob * (nt(grad[0:rows], keyval) - delta_col)
+    keyabs = nt(keyval, put_key).astype(BF16)
+    dquery = (nn(dscore.astype(BF16), keyabs) * scale).astype(BF16)
+
+    own = keyval[0:rows]
+    key_pos = positions(span_ref, here, rows, 0)
+    query_pos = jnp.concatenate([positions(span_ref, s, rows, 1) for s in query_shards], axis=1)
+    scores = nt(own, spread) * (scale * log2e)
+    prob = jnp.where(key_pos <= query_pos, jnp.exp2(scores - lse_row * log2e), F32(0.0))
+    dscore = prob * (nt(own, grad) - delta_row)
+    dkv = nn(dscore.astype(BF16), spread) * scale + nn(prob.astype(BF16), grad)
+    dkv = dkv.astype(BF16)
+    if mine is None:
+        outs[0][:, 0:width] = dquery
+        outs[0][:, width:] = dkv
+        return
+    send_ref, keep_ref = outs
+    half = send_ref.shape[0]
+    chosen = chosen_rows(mine, rows, half // 2)
+    picked = nn(chosen, dquery).astype(BF16)
+    send_ref[:, 0:width] = picked[0:half]
+    keep_ref[:, 0:width] = picked[half:]
+    picked = nn(chosen, dkv)
+    keep_ref[:, width:] = picked[half:].astype(BF16)
+    for step in (0, 1):
+        lanes = slice(step * width, (step + 1) * width)
+        rolled = pltpu.roll(picked[0:half, lanes], width // 2, 1).astype(BF16)
+        send_ref[:, (step + 1) * width : (step + 2) * width] = rolled
+
+
+def term_kernel(at, cuts, keep_ref, got_ref, wq_ref, wq2_ref, *refs):
+    weights, outs = refs[: -len(cuts)], refs[-len(cuts) :]
     width = wq_ref.shape[1]
     padded = keep_ref.shape[0] // 2
     part = slice(at * padded, (at + 1) * padded)
-    keep = keep_ref[part, :]
-    got = got_ref[part, :]
-    both = (keep[:, width:].astype(F32) + got[:, width:].astype(F32)).astype(BF16)
-    cut = depth // CUTS
-    for k in range(CUTS):
-        cols = slice(k * cut, (k + 1) * cut)
-        total = nt(keep[:, 0:width], wq_ref[cols, :]) + nt(got[:, 0:width], wq2_ref[cols, :])
-        stacked = jnp.concatenate([w[:, cols] for w in weights], axis=0)
-        total = total + nn(both, stacked)
-        out_ref[:, cols] = total[0:mine, :].astype(out_ref.dtype)
+    keep, got = keep_ref[part, 0:width], got_ref[part, 0:width]
+    both = keep_ref[part, width:].astype(F32) + got_ref[part, width:].astype(F32)
+    both = both.astype(BF16)
+    for (start, stop), out_ref in zip(cuts, outs):
+        mine = out_ref.shape[0]
+        cut = (stop - start) // 2
+        for k in range(2):
+            cols = slice(start + k * cut, start + (k + 1) * cut)
+            total = nt(keep, wq_ref[cols, :]) + nt(got, wq2_ref[cols, :])
+            stacked = jnp.concatenate([w[:, cols] for w in weights], axis=0)
+            total = total + nn(both, stacked)
+            out_ref[:, k * cut : (k + 1) * cut] = total[0:mine, :].astype(out_ref.dtype)
+
+
+def add_kernel(*refs):
+    count = (len(refs) - 1) // 2
+    stays, arrivals, out_ref = refs[:count], refs[count:-1], refs[-1]
+    at = 0
+    for stay, arrived in zip(stays, arrivals):
+        cols = slice(at, at + stay.shape[1])
+        out_ref[:, cols] = (stay[...] + arrived[...].astype(F32)).astype(BF16)
+        at += stay.shape[1]
 
 
 def per_device(
@@ -322,26 +343,35 @@
     kvx2 = flipped(kva2, "head", 2)
     wkv4 = flipped(wkv3, "head", 1)
     weights = (wkv, kw2, vw2, wkv3, wkv4)
+    fast = heads == GROUP
+    mine = rows // heads if fast else None
+    tall = 2 * (-(-rows // heads // 8) * 8)
+    outs = (((tall, 3 * width), BF16),) * 2 if fast else [((rows, 3 * width), BF16)]
     grads = local(
-        attention_kernel,
-        [((rows, 3 * width), BF16)],
+        functools.partial(attention_kernel, mine),
+        outs,
         (span_order, side, near, far, later, kva1, kvx1, kva2, kvx2),
         [pltpu.SMEM] + [pltpu.VMEM] * 8,
     )
-    if heads != GROUP:
+    if not fast:
         full = nt(grads[:, :width], query_weight)
         full = full + nn(grads[:, width:], jnp.concatenate(weights, axis=0))
         return lax.psum_scatter(full.astype(BF16), "head", scatter_dimension=0, tiled=True)
-    mine = rows // heads
-    padded = -(-mine // 8) * 8
-    block = ((2 * padded, 3 * width), BF16)
-    send, keep = local(functools.partial(split_kernel, mine), (block, block), (grads,))
+    send, keep = grads
     got = flipped(send, "head", 1)
     operands = (keep, got, query_weight, wq2) + weights
-    away = local(functools.partial(term_kernel, 0), [((mine, depth), BF16)], operands)
-    arrived = flipped(away, "head", 2)
-    stay = local(functools.partial(term_kernel, 1), [((mine, depth), F32)], operands)
-    return (stay + arrived.astype(F32)).astype(BF16)
+    half = depth // 2
+    halves = ((0, half), (half, depth))
+    arrived = []
+    for cut in halves:
+        away = local(functools.partial(term_kernel, 0, (cut,)), [((mine, half), BF16)], operands)
+        arrived.append(flipped(away, "head", 2))
+    stays = local(
+        functools.partial(term_kernel, 1, halves),
+        (((mine, half), F32), ((mine, half), F32)),
+        operands,
+    )
+    return local(add_kernel, [((mine, depth), BF16)], tuple(stays) + tuple(arrived))
 
 
 def solution(mesh):

time: 58 us -> 56.7 us (0.978)
  waiting for transfers between devices: 32.8 us -> 30.9 us
  starting transfers between devices: 16.1 us -> 17.4 us
  other arithmetic: 0.78 us -> 0 us
    ppermute x14 -> x15, waiting for transfers between devices: 32.8 us -> 30.9 us  [sent(): lax.ppermute(array, axis, [(i, to(i)) for i in range(lax.axis_size(axis))])]
    ppermute x14 -> x15, starting transfers between devices: 16.1 us -> 17.4 us  [sent(): lax.ppermute(array, axis, [(i, to(i)) for i in range(lax.axis_size(axis))])]
    convert_element_type x1 -> x0, other arithmetic: 0.78 us -> none  [per_device(): return (stay + arrived.astype(F32)).astype(BF16)]
    pallas_call x9 -> x10, Pallas kernels: 8.01 us -> 8.12 us  [local(): pl.pallas_call(body, out_shape=shapes, in_specs=[pl.BlockSpec(memory_spac...]
  transfers between devices with their start and end apart: 14 -> 15, of which waited for: 8 -> 9; matrix products, arithmetic and copies ran while one was open for 0% -> 0% of each run, Pallas kernels for 12% -> 12%
where the time goes in v1:
time: 56.7 us; the launch traced here: 56.5 us
  waiting for transfers between devices  30.9 us (54%)
  starting transfers between devices  17.4 us (31%)
  Pallas kernels  8.12 us (14%)
    ppermute x15, waiting for transfers between devices, sent(): lax.ppermute(array, axis, [(i, to(i)) for i in range(lax.axis_size(axis))])  30.9 us
    ppermute x15, starting transfers between devices, sent(): lax.ppermute(array, axis, [(i, to(i)) for i in range(lax.axis_size(axis))])  17.4 us
    pallas_call x10, Pallas kernels, local(): pl.pallas_call(body, out_shape=shapes, in_specs=[pl.BlockSpec(memory_spac...  8.12 us
  transfers between devices with their start and end apart: 15, of which 9 were waited for; matrix products, arithmetic and copies ran while one was open for 0% of the time, Pallas kernels for 12%

profile of v1, /device:TPU:0, one launch (start us, length us, event | category | flops | bytes accessed | tf_op | source)
XLA Modules:
  0.0 56.5 jit_solution(16859641704921832219)
XLA Ops:
  0.0 0.5 collective-permute-start.10
  0.5 0.0 copy-start.2
  0.5 0.0 copy-start.3
  0.5 2.3 %shard_map.82 = (bf16[152,256]{1,0:T(8,128)(2,1)S(1)}, bf16[144,4096]{1,0:T(8,128)(2,1)S(1)}, bf16[64,4096]{1,0:T(8,128)(2,1)S(1)}) custom-call(bf16[144,4096]{1,0:T(8,128)(2,1)} %norm_hbm.1, bf16[4096,128]{1,0:T(8,128)(2,1)} %wq_ref.5, bf16[32,4096]{1,0:T(8,128)(2,1)} %bitcast.2, bf16[32,4096]{1,0:T(8,128)(2,1)} %bitcast.4, bf16[144,128]{1,0:T(8,128)(2,1)} %grad_hbm.1, ...), custom_call_target="tpu_custom_call" | custom-call | tf_op jit(solution)/shard_map/pallas_call | solution.py:138
  2.8 2.5 %collective-permute-start.11 = (bf16[64,4096]{1,0:T(8,128)(2,1)S(1)}, bf16[64,4096]{1,0:T(8,128)(2,1)S(1)}, u32[]{:S(2)}, u32[]{:S(2)}) collective-permute-start(bf16[64,4096]{1,0:T(8,128)(2,1)S(1)} %get-tuple-element.16.wkv_ref.refs_0_), channel_id=1, source_target_pairs={{0,2},{1,3},{2,0},{3,1},{4,6},{5,7},{6,4},{7,5},{8,10},{9,11},{10,... | collective-permute-start | bytes 1572872 | tf_op jit(solution)/shard_map/ppermute | solution.py:302
  5.4 12.6 %collective-permute-done.11.refs_3_ = bf16[64,4096]{1,0:T(8,128)(2,1)S(1)} collective-permute-done((bf16[64,4096]{1,0:T(8,128)(2,1)S(1)}, bf16[64,4096]{1,0:T(8,128)(2,1)S(1)}, u32[]{:S(2)}, u32[]{:S(2)}) %collective-permute-start.11) | collective-permute-done | bytes 524320 | tf_op jit(solution)/shard_map/ppermute | solution.py:302
  18.0 0.0 collective-permute-start.12
  18.0 0.0 copy-done.2
  18.0 0.5 collective-permute-start.1
  18.5 0.0 copy-done.3
  18.5 0.1 collective-permute-start.2
  18.6 1.8 %collective-permute-start = (bf16[152,256]{1,0:T(8,128)(2,1)S(1)}, bf16[152,256]{1,0:T(8,128)(2,1)S(1)}, u32[]{:S(2)}, u32[]{:S(2)}) collective-permute-start(bf16[152,256]{1,0:T(8,128)(2,1)S(1)} %get-tuple-element.14.side_ref.refs_0_), channel_id=1, source_target_pairs={{0,4},{4,0},{8,12},{12,8},{16,20},{20,16},{24,28},{28,24},{1,5},{5... | collective-permute-start | bytes 233480 | tf_op jit(solution)/shard_map/ppermute | solution.py:302
  20.3 0.0 collective-permute-done.1.kw2_ref.refs_1_
  20.3 0.3 collective-permute-done.2.vw2_ref.refs_2_
  20.6 0.0 copy-start.1
  20.6 0.5 shard_map.83
  21.1 0.0 copy-start
  21.1 1.8 %collective-permute-start.5 = (bf16[144,128]{1,0:T(8,128)(2,1)S(1)}, bf16[144,128]{1,0:T(8,128)(2,1)S(1)}, u32[]{:S(2)}, u32[]{:S(2)}) collective-permute-start(bf16[144,128]{1,0:T(8,128)(2,1)S(1)} %get-tuple-element.18.own_ref.refs_0_), channel_id=1, source_target_pairs={{0,4},{4,0},{8,12},{12,8},{16,20},{20,16},{24,28},{28,24},{1,5},{5... | collective-permute-start | bytes 110600 | tf_op jit(solution)/shard_map/ppermute | solution.py:302
  23.0 0.3 collective-permute-done.refs_1_.near_ref
  23.3 3.9 %collective-permute-start.4 = (bf16[304,256]{1,0:T(8,128)(2,1)S(1)}, bf16[304,256]{1,0:T(8,128)(2,1)S(1)}, u32[]{:S(2)}, u32[]{:S(2)}) collective-permute-start(bf16[304,256]{1,0:T(8,128)(2,1)S(1)} %shard_map.84), channel_id=1, source_target_pairs={{0,24},{4,28},{8,0},{12,4},{16,8},{20,12},{24,16},{28,20},{1,25},{... | collective-permute-start | bytes 466952 | tf_op jit(solution)/shard_map/ppermute | solution.py:302
  27.2 0.4 collective-permute-start.3
  27.6 0.0 collective-permute-done.5.near_ref.refs_1_
  27.6 1.6 %collective-permute-start.7 = (bf16[288,128]{1,0:T(8,128)(2,1)S(1)}, bf16[288,128]{1,0:T(8,128)(2,1)S(1)}, u32[]{:S(2)}, u32[]{:S(2)}) collective-permute-start(bf16[288,128]{1,0:T(8,128)(2,1)S(1)} %shard_map.86), channel_id=1, source_target_pairs={{0,8},{4,12},{8,16},{12,20},{16,24},{20,28},{24,0},{28,4},{1,9},{5... | collective-permute-start | bytes 221192 | tf_op jit(solution)/shard_map/ppermute | solution.py:302
  29.2 6.8 %collective-permute-done.3.far_ref = bf16[152,256]{1,0:T(8,128)(2,1)S(1)} collective-permute-done((bf16[152,256]{1,0:T(8,128)(2,1)S(1)}, bf16[152,256]{1,0:T(8,128)(2,1)S(1)}, u32[]{:S(2)}, u32[]{:S(2)}) %collective-permute-start.3) | collective-permute-done | bytes 77856 | tf_op jit(solution)/shard_map/ppermute | solution.py:302
  36.0 1.6 %collective-permute-start.6 = (bf16[288,128]{1,0:T(8,128)(2,1)S(1)}, bf16[288,128]{1,0:T(8,128)(2,1)S(1)}, u32[]{:S(2)}, u32[]{:S(2)}) collective-permute-start(bf16[288,128]{1,0:T(8,128)(2,1)S(1)} %shard_map.85.kva1_ref), channel_id=1, source_target_pairs={{0,2},{1,3},{2,0},{3,1},{4,6},{5,7},{6,4},{7,5},{8,10},{9,11},{10,... | collective-permute-start | bytes 221192 | tf_op jit(solution)/shard_map/ppermute | solution.py:302
  37.6 0.0 collective-permute-done.7.kva2_ref
  37.6 0.5 collective-permute-start.8
  38.1 0.0 collective-permute-done.4.later_ref
  38.1 2.3 %collective-permute-done.6.kvx1_ref = bf16[288,128]{1,0:T(8,128)(2,1)S(1)} collective-permute-done((bf16[288,128]{1,0:T(8,128)(2,1)S(1)}, bf16[288,128]{1,0:T(8,128)(2,1)S(1)}, u32[]{:S(2)}, u32[]{:S(2)}) %collective-permute-start.6) | collective-permute-done | bytes 73760 | tf_op jit(solution)/shard_map/ppermute | solution.py:302
  40.4 1.5 %collective-permute-done.8.kvx2_ref = bf16[288,128]{1,0:T(8,128)(2,1)S(1)} collective-permute-done((bf16[288,128]{1,0:T(8,128)(2,1)S(1)}, bf16[288,128]{1,0:T(8,128)(2,1)S(1)}, u32[]{:S(2)}, u32[]{:S(2)}) %collective-permute-start.8) | collective-permute-done | bytes 73760 | tf_op jit(solution)/shard_map/ppermute | solution.py:302
  41.9 0.0 copy-done.1
  41.9 2.0 %shard_map.87 = (bf16[80,384]{1,0:T(8,128)(2,1)S(1)}, bf16[80,384]{1,0:T(8,128)(2,1)S(1)}) custom-call(s32[16]{0:T(128)S(1)} %copy-done.1, bf16[152,256]{1,0:T(8,128)(2,1)S(1)} %get-tuple-element.14.side_ref.refs_0_, bf16[152,256]{1,0:T(8,128)(2,1)S(1)} %collective-permute-done.refs_1_.near_ref, bf16[152,256]{1,0:T(8,128)(2,1)S(1)} %collective-permute-done.3.far_ref, ...), custom_call_target="tpu_custom_call" | custom-call | tf_op jit(solution)/shard_map/pallas_call | solution.py:138
  43.9 0.1 collective-permute-start.9
  44.0 1.2 %collective-permute-done.9.got_ref = bf16[80,384]{1,0:T(8,128)(2,1)S(1)} collective-permute-done((bf16[80,384]{1,0:T(8,128)(2,1)S(1)}, bf16[80,384]{1,0:T(8,128)(2,1)S(1)}, u32[]{:S(2)}, u32[]{:S(2)}) %collective-permute-start.9) | collective-permute-done | bytes 61472 | tf_op jit(solution)/shard_map/ppermute | solution.py:302
  45.2 0.0 collective-permute-done.10.wq2_ref
  45.2 0.0 collective-permute-done.12.refs_4_
  45.2 0.0 copy-done
  45.2 0.7 %shard_map.89 = bf16[36,2048]{1,0:T(8,128)(2,1)S(1)} custom-call(bf16[80,384]{1,0:T(8,128)(2,1)S(1)} %get-tuple-element.19.keep_ref, bf16[80,384]{1,0:T(8,128)(2,1)S(1)} %collective-permute-done.9.got_ref, bf16[4096,128]{1,0:T(8,128)(2,1)S(1)} %copy-done, bf16[4096,128]{1,0:T(8,128)(2,1)S(1)} %collective-permute-done.10.wq2_ref, ...), custom_call_target="tpu_custom_call" | custom-call | tf_op jit(solution)/shard_map/pallas_call | solution.py:138
  45.9 0.9 %collective-permute-start.13 = (bf16[36,2048]{1,0:T(8,128)(2,1)S(1)}, bf16[36,2048]{1,0:T(8,128)(2,1)S(1)}, u32[]{:S(2)}, u32[]{:S(2)}) collective-permute-start(bf16[36,2048]{1,0:T(8,128)(2,1)S(1)} %shard_map.89), channel_id=1, source_target_pairs={{0,2},{1,3},{2,0},{3,1},{4,6},{5,7},{6,4},{7,5},{8,10},{9,11},{10,... | collective-permute-start | bytes 442376 | tf_op jit(solution)/shard_map/ppermute | solution.py:302
  46.7 0.7 %shard_map.90 = bf16[36,2048]{1,0:T(8,128)(2,1)S(1)} custom-call(bf16[80,384]{1,0:T(8,128)(2,1)S(1)} %get-tuple-element.19.keep_ref, bf16[80,384]{1,0:T(8,128)(2,1)S(1)} %collective-permute-done.9.got_ref, bf16[4096,128]{1,0:T(8,128)(2,1)S(1)} %copy-done, bf16[4096,128]{1,0:T(8,128)(2,1)S(1)} %collective-permute-done.10.wq2_ref, ...), custom_call_target="tpu_custom_call" | custom-call | tf_op jit(solution)/shard_map/pallas_call | solution.py:138
  47.4 1.3 %collective-permute-start.14 = (bf16[36,2048]{1,0:T(8,128)(2,1)S(1)}, bf16[36,2048]{1,0:T(8,128)(2,1)S(1)}, u32[]{:S(2)}, u32[]{:S(2)}) collective-permute-start(bf16[36,2048]{1,0:T(8,128)(2,1)S(1)} %shard_map.90), channel_id=1, source_target_pairs={{0,2},{1,3},{2,0},{3,1},{4,6},{5,7},{6,4},{7,5},{8,10},{9,11},{10,... | collective-permute-start | bytes 442376 | tf_op jit(solution)/shard_map/ppermute | solution.py:302
  48.7 1.2 %shard_map.88 = (f32[36,2048]{1,0:T(8,128)S(1)}, f32[36,2048]{1,0:T(8,128)S(1)}) custom-call(bf16[80,384]{1,0:T(8,128)(2,1)S(1)} %get-tuple-element.19.keep_ref, bf16[80,384]{1,0:T(8,128)(2,1)S(1)} %collective-permute-done.9.got_ref, bf16[4096,128]{1,0:T(8,128)(2,1)S(1)} %copy-done, bf16[4096,128]{1,0:T(8,128)(2,1)S(1)} %collective-permute-done.10.wq2_ref, ...), custom_call_target="tpu_custom_call" | custom-call | tf_op jit(solution)/shard_map/pallas_call | solution.py:138
  49.9 3.1 %collective-permute-done.13.refs_2_ = bf16[36,2048]{1,0:T(8,128)(2,1)S(1)} collective-permute-done((bf16[36,2048]{1,0:T(8,128)(2,1)S(1)}, bf16[36,2048]{1,0:T(8,128)(2,1)S(1)}, u32[]{:S(2)}, u32[]{:S(2)}) %collective-permute-start.13) | collective-permute-done | bytes 147488 | tf_op jit(solution)/shard_map/ppermute | solution.py:302
  53.0 2.7 %collective-permute-done.14.refs_3_ = bf16[36,2048]{1,0:T(8,128)(2,1)S(1)} collective-permute-done((bf16[36,2048]{1,0:T(8,128)(2,1)S(1)}, bf16[36,2048]{1,0:T(8,128)(2,1)S(1)}, u32[]{:S(2)}, u32[]{:S(2)}) %collective-permute-start.14) | collective-permute-done | bytes 147488 | tf_op jit(solution)/shard_map/ppermute | solution.py:302
  55.7 0.8 %shard_map.91 = bf16[36,4096]{1,0:T(8,128)(2,1)} custom-call(f32[36,2048]{1,0:T(8,128)S(1)} %get-tuple-element.21.refs_0_, f32[36,2048]{1,0:T(8,128)S(1)} %get-tuple-element.22.refs_1_, bf16[36,2048]{1,0:T(8,128)(2,1)S(1)} %collective-permute-done.13.refs_2_, bf16[36,2048]{1,0:T(8,128)(2,1)S(1)} %collective-permute-done.14.refs_3_), custom_call_target="tpu_custom_call" | custom-call | tf_op jit(solution)/shard_map/pallas_call | solution.py:138
  (3 shorter events, 0.0 us)
Async XLA Ops:
  0.0 45.2 %collective-permute-start.10 = (bf16[4096,128]{1,0:T(8,128)(2,1)}, bf16[4096,128]{1,0:T(8,128)(2,1)S(1)}, u32[]{:S(2)}, u32[]{:S(2)}) collective-permute-start(bf16[4096,128]{1,0:T(8,128)(2,1)} %wq_ref.5), channel_id=1, source_target_pairs={{0,1},{1,0},{2,3},{3,2},{4,5},{5,4},{6,7},{7,6},{8,9},{9,8},{10,11... | collective-permute-start | bytes 3145736 | tf_op jit(solution)/shard_map/ppermute | solution.py:302
  0.5 17.5 %copy-start.2 = (bf16[4096,32]{0,1:T(8,128)(2,1)S(1)}, bf16[4096,32]{0,1:T(8,128)(2,1)}, u32[]{:S(2)}) copy-start(bf16[4096,32]{0,1:T(8,128)(2,1)} %param.13) | copy-start | bytes 786436
  0.5 18.0 %copy-start.3 = (bf16[4096,32]{0,1:T(8,128)(2,1)S(1)}, bf16[4096,32]{0,1:T(8,128)(2,1)}, u32[]{:S(2)}) copy-start(bf16[4096,32]{0,1:T(8,128)(2,1)} %param.14) | copy-start | bytes 786436
  2.8 15.1 %collective-permute-start.11 = (bf16[64,4096]{1,0:T(8,128)(2,1)S(1)}, bf16[64,4096]{1,0:T(8,128)(2,1)S(1)}, u32[]{:S(2)}, u32[]{:S(2)}) collective-permute-start(bf16[64,4096]{1,0:T(8,128)(2,1)S(1)} %get-tuple-element.16.wkv_ref.refs_0_), channel_id=1, source_target_pairs={{0,2},{1,3},{2,0},{3,1},{4,6},{5,7},{6,4},{7,5},{8,10},{9,11},{10,... | collective-permute-start | bytes 1572872 | tf_op jit(solution)/shard_map/ppermute | solution.py:302
  18.0 27.2 %collective-permute-start.12 = (bf16[64,4096]{1,0:T(8,128)(2,1)S(1)}, bf16[64,4096]{1,0:T(8,128)(2,1)S(1)}, u32[]{:S(2)}, u32[]{:S(2)}) collective-permute-start(bf16[64,4096]{1,0:T(8,128)(2,1)S(1)} %collective-permute-done.11.refs_3_), channel_id=1, source_target_pairs={{0,1},{1,0},{2,3},{3,2},{4,5},{5,4},{6,7},{7,6},{8,9},{9,8},{10,11... | collective-permute-start | bytes 1572872 | tf_op jit(solution)/shard_map/ppermute | solution.py:302
  18.0 2.4 %collective-permute-start.1 = (bf16[32,4096]{1,0:T(8,128)(2,1)S(1)}, bf16[32,4096]{1,0:T(8,128)(2,1)S(1)}, u32[]{:S(2)}, u32[]{:S(2)}) collective-permute-start(bf16[32,4096]{1,0:T(8,128)(2,1)S(1)} %bitcast.3), channel_id=1, source_target_pairs={{0,1},{1,0},{2,3},{3,2},{4,5},{5,4},{6,7},{7,6},{8,9},{9,8},{10,11... | collective-permute-start | bytes 786440 | tf_op jit(solution)/shard_map/ppermute | solution.py:302
  18.5 2.1 %collective-permute-start.2 = (bf16[32,4096]{1,0:T(8,128)(2,1)S(1)}, bf16[32,4096]{1,0:T(8,128)(2,1)S(1)}, u32[]{:S(2)}, u32[]{:S(2)}) collective-permute-start(bf16[32,4096]{1,0:T(8,128)(2,1)S(1)} %bitcast.5), channel_id=1, source_target_pairs={{0,1},{1,0},{2,3},{3,2},{4,5},{5,4},{6,7},{7,6},{8,9},{9,8},{10,11... | collective-permute-start | bytes 786440 | tf_op jit(solution)/shard_map/ppermute | solution.py:302
  18.6 4.7 %collective-permute-start = (bf16[152,256]{1,0:T(8,128)(2,1)S(1)}, bf16[152,256]{1,0:T(8,128)(2,1)S(1)}, u32[]{:S(2)}, u32[]{:S(2)}) collective-permute-start(bf16[152,256]{1,0:T(8,128)(2,1)S(1)} %get-tuple-element.14.side_ref.refs_0_), channel_id=1, source_target_pairs={{0,4},{4,0},{8,12},{12,8},{16,20},{20,16},{24,28},{28,24},{1,5},{5... | collective-permute-start | bytes 233480 | tf_op jit(solution)/shard_map/ppermute | solution.py:302
  20.6 21.3 %copy-start.1 = (s32[16]{0:T(128)S(1)}, s32[16]{0:T(128)}, u32[]{:S(2)}) copy-start(s32[16]{0:T(128)} %span_ref.1) | copy-start | bytes 196
  21.1 24.1 %copy-start = (bf16[4096,128]{1,0:T(8,128)(2,1)S(1)}, bf16[4096,128]{1,0:T(8,128)(2,1)}, u32[]{:S(2)}) copy-start(bf16[4096,128]{1,0:T(8,128)(2,1)} %wq_ref.5) | copy-start | bytes 3145732
  21.1 6.4 %collective-permute-start.5 = (bf16[144,128]{1,0:T(8,128)(2,1)S(1)}, bf16[144,128]{1,0:T(8,128)(2,1)S(1)}, u32[]{:S(2)}, u32[]{:S(2)}) collective-permute-start(bf16[144,128]{1,0:T(8,128)(2,1)S(1)} %get-tuple-element.18.own_ref.refs_0_), channel_id=1, source_target_pairs={{0,4},{4,0},{8,12},{12,8},{16,20},{20,16},{24,28},{28,24},{1,5},{5... | collective-permute-start | bytes 110600 | tf_op jit(solution)/shard_map/ppermute | solution.py:302
  23.3 14.8 %collective-permute-start.4 = (bf16[304,256]{1,0:T(8,128)(2,1)S(1)}, bf16[304,256]{1,0:T(8,128)(2,1)S(1)}, u32[]{:S(2)}, u32[]{:S(2)}) collective-permute-start(bf16[304,256]{1,0:T(8,128)(2,1)S(1)} %shard_map.84), channel_id=1, source_target_pairs={{0,24},{4,28},{8,0},{12,4},{16,8},{20,12},{24,16},{28,20},{1,25},{... | collective-permute-start | bytes 466952 | tf_op jit(solution)/shard_map/ppermute | solution.py:302
  27.2 8.8 %collective-permute-start.3 = (bf16[152,256]{1,0:T(8,128)(2,1)S(1)}, bf16[152,256]{1,0:T(8,128)(2,1)S(1)}, u32[]{:S(2)}, u32[]{:S(2)}) collective-permute-start(bf16[152,256]{1,0:T(8,128)(2,1)S(1)} %get-tuple-element.17), channel_id=1, source_target_pairs={{0,20},{4,16},{8,28},{12,24},{16,4},{20,0},{24,12},{28,8},{1,21},{... | collective-permute-start | bytes 233480 | tf_op jit(solution)/shard_map/ppermute | solution.py:302
  27.6 10.0 %collective-permute-start.7 = (bf16[288,128]{1,0:T(8,128)(2,1)S(1)}, bf16[288,128]{1,0:T(8,128)(2,1)S(1)}, u32[]{:S(2)}, u32[]{:S(2)}) collective-permute-start(bf16[288,128]{1,0:T(8,128)(2,1)S(1)} %shard_map.86), channel_id=1, source_target_pairs={{0,8},{4,12},{8,16},{12,20},{16,24},{20,28},{24,0},{28,4},{1,9},{5... | collective-permute-start | bytes 221192 | tf_op jit(solution)/shard_map/ppermute | solution.py:302
  36.0 4.4 %collective-permute-start.6 = (bf16[288,128]{1,0:T(8,128)(2,1)S(1)}, bf16[288,128]{1,0:T(8,128)(2,1)S(1)}, u32[]{:S(2)}, u32[]{:S(2)}) collective-permute-start(bf16[288,128]{1,0:T(8,128)(2,1)S(1)} %shard_map.85.kva1_ref), channel_id=1, source_target_pairs={{0,2},{1,3},{2,0},{3,1},{4,6},{5,7},{6,4},{7,5},{8,10},{9,11},{10,... | collective-permute-start | bytes 221192 | tf_op jit(solution)/shard_map/ppermute | solution.py:302
  37.6 4.4 %collective-permute-start.8 = (bf16[288,128]{1,0:T(8,128)(2,1)S(1)}, bf16[288,128]{1,0:T(8,128)(2,1)S(1)}, u32[]{:S(2)}, u32[]{:S(2)}) collective-permute-start(bf16[288,128]{1,0:T(8,128)(2,1)S(1)} %collective-permute-done.7.kva2_ref), channel_id=1, source_target_pairs={{0,2},{1,3},{2,0},{3,1},{4,6},{5,7},{6,4},{7,5},{8,10},{9,11},{10,... | collective-permute-start | bytes 221192 | tf_op jit(solution)/shard_map/ppermute | solution.py:302
  43.9 1.3 %collective-permute-start.9 = (bf16[80,384]{1,0:T(8,128)(2,1)S(1)}, bf16[80,384]{1,0:T(8,128)(2,1)S(1)}, u32[]{:S(2)}, u32[]{:S(2)}) collective-permute-start(bf16[80,384]{1,0:T(8,128)(2,1)S(1)} %get-tuple-element.20), channel_id=1, source_target_pairs={{0,1},{1,0},{2,3},{3,2},{4,5},{5,4},{6,7},{7,6},{8,9},{9,8},{10,11... | collective-permute-start | bytes 184328 | tf_op jit(solution)/shard_map/ppermute | solution.py:302
  45.9 7.1 %collective-permute-start.13 = (bf16[36,2048]{1,0:T(8,128)(2,1)S(1)}, bf16[36,2048]{1,0:T(8,128)(2,1)S(1)}, u32[]{:S(2)}, u32[]{:S(2)}) collective-permute-start(bf16[36,2048]{1,0:T(8,128)(2,1)S(1)} %shard_map.89), channel_id=1, source_target_pairs={{0,2},{1,3},{2,0},{3,1},{4,6},{5,7},{6,4},{7,5},{8,10},{9,11},{10,... | collective-permute-start | bytes 442376 | tf_op jit(solution)/shard_map/ppermute | solution.py:302
  47.4 8.3 %collective-permute-start.14 = (bf16[36,2048]{1,0:T(8,128)(2,1)S(1)}, bf16[36,2048]{1,0:T(8,128)(2,1)S(1)}, u32[]{:S(2)}, u32[]{:S(2)}) collective-permute-start(bf16[36,2048]{1,0:T(8,128)(2,1)S(1)} %shard_map.90), channel_id=1, source_target_pairs={{0,2},{1,3},{2,0},{3,1},{4,6},{5,7},{6,4},{7,5},{8,10},{9,11},{10,... | collective-permute-start | bytes 442376 | tf_op jit(solution)/shard_map/ppermute | solution.py:302

commit v2 on v1

--- a/solution.py
+++ b/solution.py
@@ -10,7 +10,6 @@
 
 GROUP = 4
 EXTRA = 8
-CUTS = 4
 GRANT = 16 * 2**20
 F32 = jnp.float32
 BF16 = jnp.bfloat16
@@ -35,41 +34,42 @@
     return high, middle, rest - middle
 
 
-def first_kernel(
-    norm_hbm, wq_hbm, kw_hbm, vw_hbm, grad_hbm, attn_hbm, lse_hbm,
-    side_ref, norm_ref, wkv_ref, wq_ref, grad_ref, attn_ref, lse_ref, sems,
-):
-    rows, depth = norm_ref.shape
-    width = wq_ref.shape[1]
+def load_kernel(*refs):
+    sources, (norm_ref, wkv_ref, grad_ref, attn_ref, lse_ref, sems) = refs[:6], refs[6:]
     quarter = wkv_ref.shape[0] // 2
-    cut = depth // CUTS
-
-    def fetch(at, source, target):
-        copy = pltpu.make_async_copy(source, target, sems.at[at])
+    half = norm_ref.shape[1] // 2
+    norm, kw, vw, grad, attn, lse = sources
+    pairs = (
+        (norm.at[:, 0:half], norm_ref.at[:, 0:half]),
+        (norm.at[:, half:], norm_ref.at[:, half:]),
+        (kw, wkv_ref.at[0:quarter, :]),
+        (vw, wkv_ref.at[quarter:, :]),
+        (grad, grad_ref),
+        (attn, attn_ref),
+        (lse, lse_ref),
+    )
+    copies = [pltpu.make_async_copy(a, b, sems.at[k]) for k, (a, b) in enumerate(pairs)]
+    for copy in copies:
         copy.start()
-        return copy
-
-    norms, weights = [], []
-    for k in range(CUTS):
-        part = slice(k * cut, (k + 1) * cut)
-        norms.append(fetch(2 * k, norm_hbm.at[:, part], norm_ref.at[:, part]))
-        weights.append(fetch(2 * k + 1, wq_hbm.at[part, :], wq_ref.at[part, :]))
-    at = 2 * CUTS
-    others = [
-        fetch(at, grad_hbm, grad_ref),
-        fetch(at + 1, attn_hbm, attn_ref),
-        fetch(at + 2, lse_hbm, lse_ref),
-        fetch(at + 3, kw_hbm, wkv_ref.at[0:quarter, :]),
-        fetch(at + 4, vw_hbm, wkv_ref.at[quarter : 2 * quarter, :]),
-    ]
-    query = jnp.zeros((rows, width), F32)
-    for k in range(CUTS):
-        part = slice(k * cut, (k + 1) * cut)
-        norms[k].wait()
-        weights[k].wait()
-        query = query + nn(norm_ref[:, part], wq_ref[part, :])
-    for copy in others:
+    for copy in copies:
         copy.wait()
+
+
+def keyval_kernel(norm_ref, wkv_ref, kw2_ref, vw2_ref, keyval_ref):
+    width = keyval_ref.shape[1]
+    quarter = kw2_ref.shape[0]
+    upper = lax.axis_index("head") // 2 % 2 == 1
+    own = wkv_ref[...]
+    pair = jnp.concatenate([own[0:quarter], kw2_ref[...], own[quarter:], vw2_ref[...]], axis=0)
+    keyval = nt(norm_ref[...], pair)
+    keyval_ref[...] = jnp.where(upper, pltpu.roll(keyval, width // 2, 1), keyval).astype(BF16)
+
+
+def query_kernel(norm_ref, wq_ref, grad_ref, attn_ref, lse_ref, keyval_ref, side_ref, far_ref):
+    rows, width = grad_ref.shape
+    odd = lax.axis_index("ctx") % 2 == 1
+    core = lax.axis_index("head") % 2
+    query = nn(norm_ref[...], wq_ref[...]).astype(BF16)
     grad = grad_ref[...]
     prod = grad.astype(F32) * attn_ref[...].astype(F32)
     high = prod.astype(BF16)
@@ -80,23 +80,17 @@
     extra = jnp.zeros((EXTRA, rows), F32)
     for at, piece in enumerate(three_pieces(lse_ref[...]) + three_pieces(delta)):
         extra = jnp.where(index == at, piece, extra)
-    side_ref[0:rows, 0:width] = query.astype(BF16)
-    side_ref[0:rows, width:] = grad
+    side_ref[0:rows, width:] = reordered(grad, core ^ 2)
     side_ref[rows:, :] = jnp.zeros((EXTRA, 2 * width), BF16)
     side_ref[rows:, 0:rows] = extra.astype(BF16)
-
-
-def second_kernel(norm_ref, wkv_ref, kw2_ref, vw2_ref, side_ref, keyval_ref, far_ref):
-    rows, width = keyval_ref.shape
-    odd = lax.axis_index("ctx") % 2 == 1
-    pair = jnp.concatenate([wkv_ref[...], kw2_ref[...], vw2_ref[...]], axis=0)
-    keyval = nt(norm_ref[...], pair).astype(BF16)
-    keyval_ref[...] = keyval
+    side_ref[0:rows, 0:width] = jnp.where(
+        core == 1, swapped_quarters(query.astype(F32)), query.astype(F32)
+    ).astype(BF16)
 
     @pl.when(odd)
     def _():
-        far_ref[0:rows, 0:width] = keyval
-        far_ref[0:rows, width:] = keyval
+        far_ref[0:rows, 0:width] = keyval_ref[...]
+        far_ref[0:rows, width:] = keyval_ref[...]
         far_ref[rows:, :] = jnp.zeros((EXTRA, 2 * width), BF16)
 
     @pl.when(jnp.logical_not(odd))
@@ -150,15 +144,22 @@
     return (shard + 2 * shards) % shards
 
 
-def placing(width):
+def reordered(array, flip):
+    width = array.shape[1]
     quarter = width // GROUP
-    member = lax.axis_index("head") % GROUP
-    source = lax.broadcasted_iota(jnp.int32, (width, 2 * width), 0)
-    target = lax.broadcasted_iota(jnp.int32, (width, 2 * width), 1)
-    place = ((source // quarter) ^ member) * (2 * quarter) + source % quarter
-    put_key = jnp.where(target == place, F32(1.0), F32(0.0)).astype(BF16)
-    put_value = jnp.where(target == place + quarter, F32(1.0), F32(0.0)).astype(BF16)
-    return put_key, put_value
+    source = lax.broadcasted_iota(jnp.int32, (width, width), 0)
+    target = lax.broadcasted_iota(jnp.int32, (width, width), 1)
+    moved = ((source // quarter) ^ flip) * quarter + source % quarter
+    return nn(array, jnp.where(target == moved, F32(1.0), F32(0.0)).astype(BF16)).astype(BF16)
+
+
+def swapped_quarters(array):
+    width = array.shape[1]
+    quarter = width // GROUP
+    lane = lax.broadcasted_iota(jnp.int32, array.shape, 1)
+    left = pltpu.roll(array, width - quarter, 1)
+    right = pltpu.roll(array, quarter, 1)
+    return jnp.where((lane // quarter) % 2 == 0, left, right)
 
 
 def positions(span_ref, shard, rows, axis):
@@ -197,25 +198,24 @@
     scale = width ** (-0.5)
     log2e = 1.4426950408889634
     here = lax.axis_index("ctx")
+    head = lax.axis_index("head")
+    core, upper = head % 2, head // 2 % 2
     odd = here % 2 == 1
     flip = 1 - 2 * (here % 2)
-    put_key, put_value = placing(width)
     before, after = ring(here - 2), ring(here + 2)
     key_shards = (here, ring(jnp.where(odd, here - 1, here - 3)), before, ring(before + flip))
     query_shards = (here, ring(jnp.where(odd, here + 3, here + 1)), after, ring(after + flip))
 
-    keyval = jnp.concatenate(
-        [
-            jnp.concatenate([kva1_ref[...], kvx1_ref[...]], axis=1),
-            jnp.concatenate([kva2_ref[...], kvx2_ref[...]], axis=1),
-        ],
-        axis=0,
-    )
+    mixed = jnp.concatenate([kva1_ref[...], kva2_ref[...]], axis=0)
+    other = jnp.concatenate([kvx1_ref[...], kvx2_ref[...]], axis=0)
+    lane = lax.broadcasted_iota(jnp.int32, mixed.shape, 1)
+    here_first = (lane // (width // 2)) == upper
+    key = jnp.where(here_first, mixed, other)
+    value = jnp.where(here_first, other, mixed)
     third = jnp.where(odd, far_ref[...], near_ref[...])
     blocks = (side_ref[...], third, later_ref[0:padded, :], later_ref[padded:, :])
-    spread = nn(jnp.concatenate([b[0:rows, 0:width] for b in blocks], axis=0), put_key)
-    grad = nn(jnp.concatenate([b[0:rows, width:] for b in blocks], axis=0), put_value)
-    spread, grad = spread.astype(BF16), grad.astype(BF16)
+    query = jnp.concatenate([b[0:rows, 0:width] for b in blocks], axis=0)
+    grad = jnp.concatenate([b[0:rows, width:] for b in blocks], axis=0)
     tails = [b[rows:, :].astype(F32) for b in blocks]
     lse_row = jnp.concatenate([pieces_sum(t, 0, rows) for t in tails], axis=1)
     delta_row = jnp.concatenate([pieces_sum(t, 3, rows) for t in tails], axis=1)
@@ -229,36 +229,46 @@
 
     query_pos = positions(span_ref, here, rows, 0)
     key_pos = jnp.concatenate([positions(span_ref, s, rows, 1) for s in key_shards], axis=1)
-    scores = nt(spread[0:rows], keyval) * (scale * log2e)
+    scores = nt(query[0:rows], key) * (scale * log2e)
     prob = jnp.where(key_pos <= query_pos, jnp.exp2(scores - lse_col * log2e), F32(0.0))
-    dscore = prob * (nt(grad[0:rows], keyval) - delta_col)
-    keyabs = nt(keyval, put_key).astype(BF16)
-    dquery = (nn(dscore.astype(BF16), keyabs) * scale).astype(BF16)
-
-    own = keyval[0:rows]
+    dscore = prob * (nt(grad[0:rows], value) - delta_col)
+    dquery = (nn(dscore.astype(BF16), key) * scale).astype(BF16)
+
     key_pos = positions(span_ref, here, rows, 0)
     query_pos = jnp.concatenate([positions(span_ref, s, rows, 1) for s in query_shards], axis=1)
-    scores = nt(own, spread) * (scale * log2e)
+    scores = nt(key[0:rows], query) * (scale * log2e)
     prob = jnp.where(key_pos <= query_pos, jnp.exp2(scores - lse_row * log2e), F32(0.0))
-    dscore = prob * (nt(own, grad) - delta_row)
-    dkv = nn(dscore.astype(BF16), spread) * scale + nn(prob.astype(BF16), grad)
-    dkv = dkv.astype(BF16)
+    dscore = prob * (nt(value[0:rows], grad) - delta_row)
+    dkey = (nn(dscore.astype(BF16), query) * scale).astype(BF16)
+    dvalue = nn(prob.astype(BF16), grad).astype(BF16)
+
+    def placed(array, step):
+        if step == 0:
+            return jnp.where(core == 1, swapped_quarters(array), array)
+        return jnp.where(upper == 2 - step, pltpu.roll(array, width // 2, 1), array)
+
+    results = (dquery, dkey, dvalue)
     if mine is None:
-        outs[0][:, 0:width] = dquery
-        outs[0][:, width:] = dkv
+        for step, result in enumerate(results):
+            lanes = slice(step * width, (step + 1) * width)
+            outs[0][:, lanes] = placed(result.astype(F32), step).astype(BF16)
         return
     send_ref, keep_ref = outs
     half = send_ref.shape[0]
     chosen = chosen_rows(mine, rows, half // 2)
-    picked = nn(chosen, dquery).astype(BF16)
-    send_ref[:, 0:width] = picked[0:half]
-    keep_ref[:, 0:width] = picked[half:]
-    picked = nn(chosen, dkv)
-    keep_ref[:, width:] = picked[half:].astype(BF16)
-    for step in (0, 1):
+    for step, result in enumerate(results):
         lanes = slice(step * width, (step + 1) * width)
-        rolled = pltpu.roll(picked[0:half, lanes], width // 2, 1).astype(BF16)
-        send_ref[:, (step + 1) * width : (step + 2) * width] = rolled
+        picked = placed(nn(chosen, result), step)
+        sent = picked[0:half]
+        send_ref[:, lanes] = (sent if step == 0 else swapped_quarters(sent)).astype(BF16)
+        keep_ref[:, lanes] = picked[half:].astype(BF16)
+
+
+def ordered(weights):
+    own, kw2, vw2, far, far2 = weights
+    quarter = kw2.shape[0]
+    keys = [own[0:quarter], kw2, far[0:quarter], far2[0:quarter]]
+    return keys + [own[quarter:], vw2, far[quarter:], far2[quarter:]]
 
 
 def term_kernel(at, cuts, keep_ref, got_ref, wq_ref, wq2_ref, *refs):
@@ -275,7 +285,7 @@
         for k in range(2):
             cols = slice(start + k * cut, start + (k + 1) * cut)
             total = nt(keep, wq_ref[cols, :]) + nt(got, wq2_ref[cols, :])
-            stacked = jnp.concatenate([w[:, cols] for w in weights], axis=0)
+            stacked = jnp.concatenate(ordered([w[:, cols] for w in weights]), axis=0)
             total = total + nn(both, stacked)
             out_ref[:, k * cut : (k + 1) * cut] = total[0:mine, :].astype(out_ref.dtype)
 
@@ -312,26 +322,27 @@
     kw2, vw2 = flipped(kw, "head", 1), flipped(vw, "head", 1)
     wq2 = flipped(query_weight, "head", 1)
     tall = rows + EXTRA
-    side, norm, wkv = local(
-        first_kernel,
-        (((tall, 2 * width), BF16), ((rows, depth), BF16), ((2 * quarter, depth), BF16)),
-        (norm_out, query_weight, kw, vw, out_grad, attn_out, log_norm),
-        [pltpu.HBM] * 7,
-        [
-            pltpu.VMEM((depth, width), BF16),
-            pltpu.VMEM((rows, width), BF16),
-            pltpu.VMEM((rows, width), BF16),
-            pltpu.VMEM((1, rows), F32),
-            pltpu.SemaphoreType.DMA((2 * CUTS + 5,)),
-        ],
+    norm, wkv, grad, attn, lse = local(
+        load_kernel,
+        (
+            ((rows, depth), BF16),
+            ((2 * quarter, depth), BF16),
+            ((rows, width), BF16),
+            ((rows, width), BF16),
+            ((1, rows), F32),
+        ),
+        (norm_out, kw, vw, out_grad, attn_out, log_norm),
+        [pltpu.HBM] * 6,
+        [pltpu.SemaphoreType.DMA((7,))],
     )
     wkv3 = flipped(wkv, "head", 2)
-    keyval, far = local(
-        second_kernel,
-        (((rows, width), BF16), ((tall, 2 * width), BF16)),
-        (norm, wkv, kw2, vw2, side),
-    )
+    keyval = local(keyval_kernel, [((rows, width), BF16)], (norm, wkv, kw2, vw2))
     near_kv = flipped(keyval, "ctx", 1)
+    side, far = local(
+        query_kernel,
+        (((tall, 2 * width), BF16), ((tall, 2 * width), BF16)),
+        (norm, query_weight, grad, attn, lse, keyval),
+    )
     near = flipped(side, "ctx", 1)
     far = sent(far, "ctx", lambda i: (i + (3 if i % 2 else -3)) % shards)
     pair_kv = local(stack_kernel, [((2 * rows, width), BF16)], (keyval, near_kv))
@@ -355,7 +366,7 @@
     )
     if not fast:
         full = nt(grads[:, :width], query_weight)
-        full = full + nn(grads[:, width:], jnp.concatenate(weights, axis=0))
+        full = full + nn(grads[:, width:], jnp.concatenate(ordered(weights), axis=0))
         return lax.psum_scatter(full.astype(BF16), "head", scatter_dimension=0, tiled=True)
     send, keep = grads
     got = flipped(send, "head", 1)

time: 56.7 us -> 56.2 us (level)
  waiting for transfers between devices: 30.9 us -> 32.4 us
  starting transfers between devices: 17.4 us -> 16.1 us
  Pallas kernels: 8.12 us -> 7.49 us
    ppermute x15, waiting for transfers between devices: 30.9 us -> 32.4 us  [sent(): lax.ppermute(array, axis, [(i, to(i)) for i in range(lax.axis_size(axis))])]
    ppermute x15, starting transfers between devices: 17.4 us -> 16.1 us  [sent(): lax.ppermute(array, axis, [(i, to(i)) for i in range(lax.axis_size(axis))])]
    pallas_call x10 -> x11, Pallas kernels: 8.12 us -> 7.49 us  [local(): pl.pallas_call(body, out_shape=shapes, in_specs=[pl.BlockSpec(memory_spac...]
  transfers between devices with their start and end apart: 15 -> 15, of which waited for: 9 -> 8; matrix products, arithmetic and copies ran while one was open for 0% -> 0% of each run, Pallas kernels for 12% -> 11%
where the time goes in v2:
time: 56.2 us; the launch traced here: 56.1 us
  waiting for transfers between devices  32.4 us (58%)
  starting transfers between devices  16.1 us (29%)
  Pallas kernels  7.49 us (13%)
    ppermute x15, waiting for transfers between devices, sent(): lax.ppermute(array, axis, [(i, to(i)) for i in range(lax.axis_size(axis))])  32.4 us
    ppermute x15, starting transfers between devices, sent(): lax.ppermute(array, axis, [(i, to(i)) for i in range(lax.axis_size(axis))])  16.1 us
    pallas_call x11, Pallas kernels, local(): pl.pallas_call(body, out_shape=shapes, in_specs=[pl.BlockSpec(memory_spac...  7.49 us
  transfers between devices with their start and end apart: 15, of which 8 were waited for; matrix products, arithmetic and copies ran while one was open for 0% of the time, Pallas kernels for 11%

profile of v2, /device:TPU:0, one launch (start us, length us, event | category | flops | bytes accessed | tf_op | source)
XLA Modules:
  0.0 56.1 jit_solution(12279939177768824318)
XLA Ops:
  0.0 0.0 copy-start.3
  0.0 0.0 copy-start.2
  0.0 0.5 collective-permute-start.10
  0.5 1.4 %shard_map.82 = (bf16[144,4096]{1,0:T(8,128)(2,1)S(1)}, bf16[64,4096]{1,0:T(8,128)(2,1)S(1)}, bf16[144,128]{1,0:T(8,128)(2,1)S(1)}, bf16[144,128]{1,0:T(8,128)(2,1)S(1)}, f32[1,144]{1,0:T(1,128)S(1)}) custom-call(bf16[144,4096]{1,0:T(8,128)(2,1)} %refs_0_.1, bf16[32,4096]{1,0:T(8,128)(2,1)} %bitcast.2, bf16[32,4096]{1,0:T(8,128)(2,1)} %bitcast.4, ...), custom_call_target="tpu_custom_call" | custom-call | tf_op jit(solution)/shard_map/pallas_call | solution.py:132
  2.0 0.0 copy-start
  2.0 2.6 %collective-permute-start.11 = (bf16[64,4096]{1,0:T(8,128)(2,1)S(1)}, bf16[64,4096]{1,0:T(8,128)(2,1)S(1)}, u32[]{:S(2)}, u32[]{:S(2)}) collective-permute-start(bf16[64,4096]{1,0:T(8,128)(2,1)S(1)} %get-tuple-element.20.wkv_ref.refs_0_), channel_id=1, source_target_pairs={{0,2},{1,3},{2,0},{3,1},{4,6},{5,7},{6,4},{7,5},{8,10},{9,11},{10,... | collective-permute-start | bytes 1572872 | tf_op jit(solution)/shard_map/ppermute | solution.py:312
  4.6 0.0 copy-done.2
  4.6 0.2 collective-permute-start
  4.7 0.0 copy-done.3
  4.7 0.3 collective-permute-start.1
  5.1 12.0 %collective-permute-done.11.refs_3_ = bf16[64,4096]{1,0:T(8,128)(2,1)S(1)} collective-permute-done((bf16[64,4096]{1,0:T(8,128)(2,1)S(1)}, bf16[64,4096]{1,0:T(8,128)(2,1)S(1)}, u32[]{:S(2)}, u32[]{:S(2)}) %collective-permute-start.11) | collective-permute-done | bytes 524320 | tf_op jit(solution)/shard_map/ppermute | solution.py:312
  17.1 0.0 collective-permute-start.12
  17.1 0.0 collective-permute-done.kw2_ref.refs_1_
  17.1 0.0 collective-permute-done.1.vw2_ref.refs_2_
  17.1 0.5 shard_map.83.keyval_ref.own_ref.refs_0_
  17.7 0.0 copy-done
  17.7 0.0 copy-start.1
  17.7 0.5 shard_map.84
  18.2 1.8 %collective-permute-start.2 = (bf16[152,256]{1,0:T(8,128)(2,1)S(1)}, bf16[152,256]{1,0:T(8,128)(2,1)S(1)}, u32[]{:S(2)}, u32[]{:S(2)}) collective-permute-start(bf16[152,256]{1,0:T(8,128)(2,1)S(1)} %get-tuple-element.21.refs_0_.side_ref), channel_id=1, source_target_pairs={{0,4},{4,0},{8,12},{12,8},{16,20},{20,16},{24,28},{28,24},{1,5},{5... | collective-permute-start | bytes 233480 | tf_op jit(solution)/shard_map/ppermute | solution.py:312
  20.1 0.3 collective-permute-start.5
  20.3 3.0 %collective-permute-done.2.refs_1_.near_ref = bf16[152,256]{1,0:T(8,128)(2,1)S(1)} collective-permute-done((bf16[152,256]{1,0:T(8,128)(2,1)S(1)}, bf16[152,256]{1,0:T(8,128)(2,1)S(1)}, u32[]{:S(2)}, u32[]{:S(2)}) %collective-permute-start.2) | collective-permute-done | bytes 77856 | tf_op jit(solution)/shard_map/ppermute | solution.py:312
  23.3 4.1 %collective-permute-start.4 = (bf16[304,256]{1,0:T(8,128)(2,1)S(1)}, bf16[304,256]{1,0:T(8,128)(2,1)S(1)}, u32[]{:S(2)}, u32[]{:S(2)}) collective-permute-start(bf16[304,256]{1,0:T(8,128)(2,1)S(1)} %shard_map.85), channel_id=1, source_target_pairs={{0,24},{4,28},{8,0},{12,4},{16,8},{20,12},{24,16},{28,20},{1,25},{... | collective-permute-start | bytes 466952 | tf_op jit(solution)/shard_map/ppermute | solution.py:312
  27.4 0.4 collective-permute-start.3
  27.8 0.0 collective-permute-done.5.near_ref.refs_1_
  27.8 1.6 %collective-permute-start.7 = (bf16[288,128]{1,0:T(8,128)(2,1)S(1)}, bf16[288,128]{1,0:T(8,128)(2,1)S(1)}, u32[]{:S(2)}, u32[]{:S(2)}) collective-permute-start(bf16[288,128]{1,0:T(8,128)(2,1)S(1)} %shard_map.87), channel_id=1, source_target_pairs={{0,8},{4,12},{8,16},{12,20},{16,24},{20,28},{24,0},{28,4},{1,9},{5... | collective-permute-start | bytes 221192 | tf_op jit(solution)/shard_map/ppermute | solution.py:312
  29.4 6.5 %collective-permute-done.3.far_ref = bf16[152,256]{1,0:T(8,128)(2,1)S(1)} collective-permute-done((bf16[152,256]{1,0:T(8,128)(2,1)S(1)}, bf16[152,256]{1,0:T(8,128)(2,1)S(1)}, u32[]{:S(2)}, u32[]{:S(2)}) %collective-permute-start.3) | collective-permute-done | bytes 77856 | tf_op jit(solution)/shard_map/ppermute | solution.py:312
  35.9 1.6 %collective-permute-start.6 = (bf16[288,128]{1,0:T(8,128)(2,1)S(1)}, bf16[288,128]{1,0:T(8,128)(2,1)S(1)}, u32[]{:S(2)}, u32[]{:S(2)}) collective-permute-start(bf16[288,128]{1,0:T(8,128)(2,1)S(1)} %shard_map.86.kva1_ref), channel_id=1, source_target_pairs={{0,2},{1,3},{2,0},{3,1},{4,6},{5,7},{6,4},{7,5},{8,10},{9,11},{10,... | collective-permute-start | bytes 221192 | tf_op jit(solution)/shard_map/ppermute | solution.py:312
  37.5 0.0 collective-permute-done.7.kva2_ref
  37.5 0.5 collective-permute-start.8
  38.0 3.0 %collective-permute-done.6.kvx1_ref = bf16[288,128]{1,0:T(8,128)(2,1)S(1)} collective-permute-done((bf16[288,128]{1,0:T(8,128)(2,1)S(1)}, bf16[288,128]{1,0:T(8,128)(2,1)S(1)}, u32[]{:S(2)}, u32[]{:S(2)}) %collective-permute-start.6) | collective-permute-done | bytes 73760 | tf_op jit(solution)/shard_map/ppermute | solution.py:312
  41.0 0.8 %collective-permute-done.8.kvx2_ref = bf16[288,128]{1,0:T(8,128)(2,1)S(1)} collective-permute-done((bf16[288,128]{1,0:T(8,128)(2,1)S(1)}, bf16[288,128]{1,0:T(8,128)(2,1)S(1)}, u32[]{:S(2)}, u32[]{:S(2)}) %collective-permute-start.8) | collective-permute-done | bytes 73760 | tf_op jit(solution)/shard_map/ppermute | solution.py:312
  41.8 0.0 collective-permute-done.4.later_ref
  41.8 0.0 copy-done.1
  41.8 1.6 %shard_map.88 = (bf16[80,384]{1,0:T(8,128)(2,1)S(1)}, bf16[80,384]{1,0:T(8,128)(2,1)S(1)}) custom-call(s32[16]{0:T(128)S(1)} %copy-done.1, bf16[152,256]{1,0:T(8,128)(2,1)S(1)} %get-tuple-element.21.refs_0_.side_ref, bf16[152,256]{1,0:T(8,128)(2,1)S(1)} %collective-permute-done.2.refs_1_.near_ref, bf16[152,256]{1,0:T(8,128)(2,1)S(1)} %collective-permute-done.3.far_ref, ...), custom_call_target="tpu_custom_call" | custom-call | tf_op jit(solution)/shard_map/pallas_call | solution.py:132
  43.5 0.1 collective-permute-start.9
  43.5 1.2 %collective-permute-done.9.got_ref = bf16[80,384]{1,0:T(8,128)(2,1)S(1)} collective-permute-done((bf16[80,384]{1,0:T(8,128)(2,1)S(1)}, bf16[80,384]{1,0:T(8,128)(2,1)S(1)}, u32[]{:S(2)}, u32[]{:S(2)}) %collective-permute-start.9) | collective-permute-done | bytes 61472 | tf_op jit(solution)/shard_map/ppermute | solution.py:312
  44.8 0.0 collective-permute-done.10.wq2_ref
  44.8 0.0 collective-permute-done.12.refs_4_
  44.8 0.7 %shard_map.90 = bf16[36,2048]{1,0:T(8,128)(2,1)S(1)} custom-call(bf16[80,384]{1,0:T(8,128)(2,1)S(1)} %get-tuple-element.23.keep_ref, bf16[80,384]{1,0:T(8,128)(2,1)S(1)} %collective-permute-done.9.got_ref, bf16[4096,128]{1,0:T(8,128)(2,1)S(1)} %copy-done, bf16[4096,128]{1,0:T(8,128)(2,1)S(1)} %collective-permute-done.10.wq2_ref, ...), custom_call_target="tpu_custom_call" | custom-call | tf_op jit(solution)/shard_map/pallas_call | solution.py:132
  45.4 1.1 %collective-permute-start.13 = (bf16[36,2048]{1,0:T(8,128)(2,1)S(1)}, bf16[36,2048]{1,0:T(8,128)(2,1)S(1)}, u32[]{:S(2)}, u32[]{:S(2)}) collective-permute-start(bf16[36,2048]{1,0:T(8,128)(2,1)S(1)} %shard_map.90), channel_id=1, source_target_pairs={{0,2},{1,3},{2,0},{3,1},{4,6},{5,7},{6,4},{7,5},{8,10},{9,11},{10,... | collective-permute-start | bytes 442376 | tf_op jit(solution)/shard_map/ppermute | solution.py:312
  46.5 0.7 %shard_map.91 = bf16[36,2048]{1,0:T(8,128)(2,1)S(1)} custom-call(bf16[80,384]{1,0:T(8,128)(2,1)S(1)} %get-tuple-element.23.keep_ref, bf16[80,384]{1,0:T(8,128)(2,1)S(1)} %collective-permute-done.9.got_ref, bf16[4096,128]{1,0:T(8,128)(2,1)S(1)} %copy-done, bf16[4096,128]{1,0:T(8,128)(2,1)S(1)} %collective-permute-done.10.wq2_ref, ...), custom_call_target="tpu_custom_call" | custom-call | tf_op jit(solution)/shard_map/pallas_call | solution.py:132
  47.2 1.1 %collective-permute-start.14 = (bf16[36,2048]{1,0:T(8,128)(2,1)S(1)}, bf16[36,2048]{1,0:T(8,128)(2,1)S(1)}, u32[]{:S(2)}, u32[]{:S(2)}) collective-permute-start(bf16[36,2048]{1,0:T(8,128)(2,1)S(1)} %shard_map.91), channel_id=1, source_target_pairs={{0,2},{1,3},{2,0},{3,1},{4,6},{5,7},{6,4},{7,5},{8,10},{9,11},{10,... | collective-permute-start | bytes 442376 | tf_op jit(solution)/shard_map/ppermute | solution.py:312
  48.3 1.2 %shard_map.89 = (f32[36,2048]{1,0:T(8,128)S(1)}, f32[36,2048]{1,0:T(8,128)S(1)}) custom-call(bf16[80,384]{1,0:T(8,128)(2,1)S(1)} %get-tuple-element.23.keep_ref, bf16[80,384]{1,0:T(8,128)(2,1)S(1)} %collective-permute-done.9.got_ref, bf16[4096,128]{1,0:T(8,128)(2,1)S(1)} %copy-done, bf16[4096,128]{1,0:T(8,128)(2,1)S(1)} %collective-permute-done.10.wq2_ref, ...), custom_call_target="tpu_custom_call" | custom-call | tf_op jit(solution)/shard_map/pallas_call | solution.py:132
  49.5 3.1 %collective-permute-done.13.refs_2_ = bf16[36,2048]{1,0:T(8,128)(2,1)S(1)} collective-permute-done((bf16[36,2048]{1,0:T(8,128)(2,1)S(1)}, bf16[36,2048]{1,0:T(8,128)(2,1)S(1)}, u32[]{:S(2)}, u32[]{:S(2)}) %collective-permute-start.13) | collective-permute-done | bytes 147488 | tf_op jit(solution)/shard_map/ppermute | solution.py:312
  52.6 2.7 %collective-permute-done.14.refs_3_ = bf16[36,2048]{1,0:T(8,128)(2,1)S(1)} collective-permute-done((bf16[36,2048]{1,0:T(8,128)(2,1)S(1)}, bf16[36,2048]{1,0:T(8,128)(2,1)S(1)}, u32[]{:S(2)}, u32[]{:S(2)}) %collective-permute-start.14) | collective-permute-done | bytes 147488 | tf_op jit(solution)/shard_map/ppermute | solution.py:312
  55.3 0.8 %shard_map.92 = bf16[36,4096]{1,0:T(8,128)(2,1)} custom-call(f32[36,2048]{1,0:T(8,128)S(1)} %get-tuple-element.25.refs_0_, f32[36,2048]{1,0:T(8,128)S(1)} %get-tuple-element.26.refs_1_, bf16[36,2048]{1,0:T(8,128)(2,1)S(1)} %collective-permute-done.13.refs_2_, bf16[36,2048]{1,0:T(8,128)(2,1)S(1)} %collective-permute-done.14.refs_3_), custom_call_target="tpu_custom_call" | custom-call | tf_op jit(solution)/shard_map/pallas_call | solution.py:132
  (3 shorter events, 0.0 us)
Async XLA Ops:
  0.0 4.7 %copy-start.3 = (bf16[4096,32]{0,1:T(8,128)(2,1)S(1)}, bf16[4096,32]{0,1:T(8,128)(2,1)}, u32[]{:S(2)}) copy-start(bf16[4096,32]{0,1:T(8,128)(2,1)} %param.14) | copy-start | bytes 786436
  0.0 4.6 %copy-start.2 = (bf16[4096,32]{0,1:T(8,128)(2,1)S(1)}, bf16[4096,32]{0,1:T(8,128)(2,1)}, u32[]{:S(2)}) copy-start(bf16[4096,32]{0,1:T(8,128)(2,1)} %param.13) | copy-start | bytes 786436
  0.0 44.8 %collective-permute-start.10 = (bf16[4096,128]{1,0:T(8,128)(2,1)}, bf16[4096,128]{1,0:T(8,128)(2,1)S(1)}, u32[]{:S(2)}, u32[]{:S(2)}) collective-permute-start(bf16[4096,128]{1,0:T(8,128)(2,1)} %wq_ref.7), channel_id=1, source_target_pairs={{0,1},{1,0},{2,3},{3,2},{4,5},{5,4},{6,7},{7,6},{8,9},{9,8},{10,11... | collective-permute-start | bytes 3145736 | tf_op jit(solution)/shard_map/ppermute | solution.py:312
  2.0 15.7 %copy-start = (bf16[4096,128]{1,0:T(8,128)(2,1)S(1)}, bf16[4096,128]{1,0:T(8,128)(2,1)}, u32[]{:S(2)}) copy-start(bf16[4096,128]{1,0:T(8,128)(2,1)} %wq_ref.7) | copy-start | bytes 3145732
  2.0 15.1 %collective-permute-start.11 = (bf16[64,4096]{1,0:T(8,128)(2,1)S(1)}, bf16[64,4096]{1,0:T(8,128)(2,1)S(1)}, u32[]{:S(2)}, u32[]{:S(2)}) collective-permute-start(bf16[64,4096]{1,0:T(8,128)(2,1)S(1)} %get-tuple-element.20.wkv_ref.refs_0_), channel_id=1, source_target_pairs={{0,2},{1,3},{2,0},{3,1},{4,6},{5,7},{6,4},{7,5},{8,10},{9,11},{10,... | collective-permute-start | bytes 1572872 | tf_op jit(solution)/shard_map/ppermute | solution.py:312
  4.6 12.5 %collective-permute-start = (bf16[32,4096]{1,0:T(8,128)(2,1)S(1)}, bf16[32,4096]{1,0:T(8,128)(2,1)S(1)}, u32[]{:S(2)}, u32[]{:S(2)}) collective-permute-start(bf16[32,4096]{1,0:T(8,128)(2,1)S(1)} %bitcast.3), channel_id=1, source_target_pairs={{0,1},{1,0},{2,3},{3,2},{4,5},{5,4},{6,7},{7,6},{8,9},{9,8},{10,11... | collective-permute-start | bytes 786440 | tf_op jit(solution)/shard_map/ppermute | solution.py:312
  4.7 12.4 %collective-permute-start.1 = (bf16[32,4096]{1,0:T(8,128)(2,1)S(1)}, bf16[32,4096]{1,0:T(8,128)(2,1)S(1)}, u32[]{:S(2)}, u32[]{:S(2)}) collective-permute-start(bf16[32,4096]{1,0:T(8,128)(2,1)S(1)} %bitcast.5), channel_id=1, source_target_pairs={{0,1},{1,0},{2,3},{3,2},{4,5},{5,4},{6,7},{7,6},{8,9},{9,8},{10,11... | collective-permute-start | bytes 786440 | tf_op jit(solution)/shard_map/ppermute | solution.py:312
  17.1 27.7 %collective-permute-start.12 = (bf16[64,4096]{1,0:T(8,128)(2,1)S(1)}, bf16[64,4096]{1,0:T(8,128)(2,1)S(1)}, u32[]{:S(2)}, u32[]{:S(2)}) collective-permute-start(bf16[64,4096]{1,0:T(8,128)(2,1)S(1)} %collective-permute-done.11.refs_3_), channel_id=1, source_target_pairs={{0,1},{1,0},{2,3},{3,2},{4,5},{5,4},{6,7},{7,6},{8,9},{9,8},{10,11... | collective-permute-start | bytes 1572872 | tf_op jit(solution)/shard_map/ppermute | solution.py:312
  17.7 24.2 %copy-start.1 = (s32[16]{0:T(128)S(1)}, s32[16]{0:T(128)}, u32[]{:S(2)}) copy-start(s32[16]{0:T(128)} %span_ref.1) | copy-start | bytes 196
  18.2 5.1 %collective-permute-start.2 = (bf16[152,256]{1,0:T(8,128)(2,1)S(1)}, bf16[152,256]{1,0:T(8,128)(2,1)S(1)}, u32[]{:S(2)}, u32[]{:S(2)}) collective-permute-start(bf16[152,256]{1,0:T(8,128)(2,1)S(1)} %get-tuple-element.21.refs_0_.side_ref), channel_id=1, source_target_pairs={{0,4},{4,0},{8,12},{12,8},{16,20},{20,16},{24,28},{28,24},{1,5},{5... | collective-permute-start | bytes 233480 | tf_op jit(solution)/shard_map/ppermute | solution.py:312
  20.1 7.7 %collective-permute-start.5 = (bf16[144,128]{1,0:T(8,128)(2,1)S(1)}, bf16[144,128]{1,0:T(8,128)(2,1)S(1)}, u32[]{:S(2)}, u32[]{:S(2)}) collective-permute-start(bf16[144,128]{1,0:T(8,128)(2,1)S(1)} %shard_map.83.keyval_ref.own_ref.refs_0_), channel_id=1, source_target_pairs={{0,4},{4,0},{8,12},{12,8},{16,20},{20,16},{24,28},{28,24},{1,5},{5... | collective-permute-start | bytes 110600 | tf_op jit(solution)/shard_map/ppermute | solution.py:312
  23.3 18.5 %collective-permute-start.4 = (bf16[304,256]{1,0:T(8,128)(2,1)S(1)}, bf16[304,256]{1,0:T(8,128)(2,1)S(1)}, u32[]{:S(2)}, u32[]{:S(2)}) collective-permute-start(bf16[304,256]{1,0:T(8,128)(2,1)S(1)} %shard_map.85), channel_id=1, source_target_pairs={{0,24},{4,28},{8,0},{12,4},{16,8},{20,12},{24,16},{28,20},{1,25},{... | collective-permute-start | bytes 466952 | tf_op jit(solution)/shard_map/ppermute | solution.py:312
  27.4 8.5 %collective-permute-start.3 = (bf16[152,256]{1,0:T(8,128)(2,1)S(1)}, bf16[152,256]{1,0:T(8,128)(2,1)S(1)}, u32[]{:S(2)}, u32[]{:S(2)}) collective-permute-start(bf16[152,256]{1,0:T(8,128)(2,1)S(1)} %get-tuple-element.22), channel_id=1, source_target_pairs={{0,20},{4,16},{8,28},{12,24},{16,4},{20,0},{24,12},{28,8},{1,21},{... | collective-permute-start | bytes 233480 | tf_op jit(solution)/shard_map/ppermute | solution.py:312
  27.8 9.7 %collective-permute-start.7 = (bf16[288,128]{1,0:T(8,128)(2,1)S(1)}, bf16[288,128]{1,0:T(8,128)(2,1)S(1)}, u32[]{:S(2)}, u32[]{:S(2)}) collective-permute-start(bf16[288,128]{1,0:T(8,128)(2,1)S(1)} %shard_map.87), channel_id=1, source_target_pairs={{0,8},{4,12},{8,16},{12,20},{16,24},{20,28},{24,0},{28,4},{1,9},{5... | collective-permute-start | bytes 221192 | tf_op jit(solution)/shard_map/ppermute | solution.py:312
  35.9 5.1 %collective-permute-start.6 = (bf16[288,128]{1,0:T(8,128)(2,1)S(1)}, bf16[288,128]{1,0:T(8,128)(2,1)S(1)}, u32[]{:S(2)}, u32[]{:S(2)}) collective-permute-start(bf16[288,128]{1,0:T(8,128)(2,1)S(1)} %shard_map.86.kva1_ref), channel_id=1, source_target_pairs={{0,2},{1,3},{2,0},{3,1},{4,6},{5,7},{6,4},{7,5},{8,10},{9,11},{10,... | collective-permute-start | bytes 221192 | tf_op jit(solution)/shard_map/ppermute | solution.py:312
  37.5 4.4 %collective-permute-start.8 = (bf16[288,128]{1,0:T(8,128)(2,1)S(1)}, bf16[288,128]{1,0:T(8,128)(2,1)S(1)}, u32[]{:S(2)}, u32[]{:S(2)}) collective-permute-start(bf16[288,128]{1,0:T(8,128)(2,1)S(1)} %collective-permute-done.7.kva2_ref), channel_id=1, source_target_pairs={{0,2},{1,3},{2,0},{3,1},{4,6},{5,7},{6,4},{7,5},{8,10},{9,11},{10,... | collective-permute-start | bytes 221192 | tf_op jit(solution)/shard_map/ppermute | solution.py:312
  43.5 1.3 %collective-permute-start.9 = (bf16[80,384]{1,0:T(8,128)(2,1)S(1)}, bf16[80,384]{1,0:T(8,128)(2,1)S(1)}, u32[]{:S(2)}, u32[]{:S(2)}) collective-permute-start(bf16[80,384]{1,0:T(8,128)(2,1)S(1)} %get-tuple-element.24), channel_id=1, source_target_pairs={{0,1},{1,0},{2,3},{3,2},{4,5},{5,4},{6,7},{7,6},{8,9},{9,8},{10,11... | collective-permute-start | bytes 184328 | tf_op jit(solution)/shard_map/ppermute | solution.py:312
  45.4 7.1 %collective-permute-start.13 = (bf16[36,2048]{1,0:T(8,128)(2,1)S(1)}, bf16[36,2048]{1,0:T(8,128)(2,1)S(1)}, u32[]{:S(2)}, u32[]{:S(2)}) collective-permute-start(bf16[36,2048]{1,0:T(8,128)(2,1)S(1)} %shard_map.90), channel_id=1, source_target_pairs={{0,2},{1,3},{2,0},{3,1},{4,6},{5,7},{6,4},{7,5},{8,10},{9,11},{10,... | collective-permute-start | bytes 442376 | tf_op jit(solution)/shard_map/ppermute | solution.py:312
  47.2 8.1 %collective-permute-start.14 = (bf16[36,2048]{1,0:T(8,128)(2,1)S(1)}, bf16[36,2048]{1,0:T(8,128)(2,1)S(1)}, u32[]{:S(2)}, u32[]{:S(2)}) collective-permute-start(bf16[36,2048]{1,0:T(8,128)(2,1)S(1)} %shard_map.91), channel_id=1, source_target_pairs={{0,2},{1,3},{2,0},{3,1},{4,6},{5,7},{6,4},{7,5},{8,10},{9,11},{10,... | collective-permute-start | bytes 442376 | tf_op jit(solution)/shard_map/ppermute | solution.py:312
